TPU v7x, 128 devices: a whole 4x4x4 slice. The times are simulated.
128 devices in a mesh: scan: 4 (over y_lo, core), ybrick: 32 (over y_hi, x, z).
Axes of the slice: x: 4, y: 4 (y_hi: 2, y_lo: 2; y = y_hi * 2 + y_lo), z: 4, core: 2. Of those that a mesh axis runs over, the one named last changes fastest.
Arguments:
- raw: bfloat16 [16, 4096, 2048], P(None, 'ybrick', 'scan'), may hold values from 0.099609375 to 4
- row_shift: int32 [16], replicated, may hold values from 0 to 1023
- frac_index: int32 [16], replicated, may hold values from 0 to 15
- psf_y: float32 [65], replicated, may hold values from 0.05 to 1
- psf_x: float32 [65], replicated, may hold values from 0.05 to 1
Outputs:
- estimate: float32 [16, 4096, 2048], P('scan', 'ybrick')
All inputs are finite; a program needn't handle non-finite values.
Results may differ from a plain program's by a relative error of at most 0.0021.
Values may be sent and summed in bfloat16 or wider, within the bound.
A program may use at most 128 MiB of HBM per device.

v0:
```python
import jax
import jax.numpy as jnp
from jax import lax
from jax.sharding import PartitionSpec as P

RADIUS = 32
ITERS = 2
NFRAC = 16


background = 0.5


def shifted_2(x, axis, by):
    devices = lax.axis_size(axis)
    pairs = [(i, i + by) for i in range(devices) if 0 <= i + by < devices]
    return lax.ppermute(x, axis, pairs)


def with_halo(x, sides, width):
    for axis, dim in sides:
        devices, length = (lax.axis_size(axis), x.shape[dim])
        up = [(i, (i + 1) % devices) for i in range(devices - 1)]
        down = [(j, i) for i, j in up]
        last = lax.slice_in_dim(x, length - width, length, axis=dim)
        initial = lax.slice_in_dim(x, 0, width, axis=dim)
        before = lax.ppermute(last, axis, up)
        after = lax.ppermute(initial, axis, down)
        x = jnp.concatenate([before, x, after], axis=dim)
    return x


def band_matrix(kernel, count_in, count_out, offset):
    inputs = jnp.arange(count_in, dtype=jnp.int32)[:, None]
    outputs = jnp.arange(count_out, dtype=jnp.int32)[None, :]
    onehot = jax.nn.one_hot(inputs - outputs + offset, kernel.shape[0], dtype=jnp.float32)
    return jnp.dot(onehot, kernel, precision=lax.Precision.HIGHEST)


def along_rows(source, matrix):
    return jnp.einsum("io,pix->pox", matrix, source, precision=lax.Precision.HIGHEST)


def along_columns(source, matrix):

    def per_frame(frame_data):
        height, width = frame_data.shape
        padded = jnp.pad(frame_data, ((0, 0), (128, 128)))
        blocks = padded.reshape(height, width // 128 + 2, 128)
        windows = jnp.concatenate([blocks[:, :-2], blocks[:, 1:-1], blocks[:, 2:]], axis=-1)
        return jnp.einsum("rbi,io->rbo", windows, matrix, precision=lax.Precision.HIGHEST).reshape(
            height, width
        )

    return lax.map(per_frame, source)


def step_bricks(moved, whole_bricks, power):
    shifted = shifted_2(moved, "ybrick", 2**power)
    taken = (whole_bricks // 2**power % 2 == 1)[:, None, None]
    return jnp.where(taken, shifted, moved)


def deskew_brick(stacked, rest, fraction, brick):
    weight = fraction.astype(jnp.float32) / NFRAC
    upper = lax.dynamic_slice_in_dim(stacked, brick - rest, brick, 0)
    lower = lax.dynamic_slice_in_dim(stacked, brick - rest - 1, brick, 0)
    return ((1.0 - weight) * upper + weight * lower).astype(jnp.bfloat16)


def local(raw, row_shift, frac_index, psf_y, psf_x):
    arranged = lax.all_to_all(raw, "scan", split_axis=0, concat_axis=2, tiled=True)
    group_planes = arranged.shape[0]
    brick = arranged.shape[1]
    first_plane = lax.axis_index("scan") * group_planes
    shifts = lax.dynamic_slice_in_dim(row_shift, first_plane, group_planes)
    fractions = lax.dynamic_slice_in_dim(frac_index, first_plane, group_planes)
    whole_bricks = shifts // brick
    rests = shifts % brick
    moved = arranged
    for power in range((lax.axis_size("ybrick") // 4 - 1).bit_length()):
        moved = step_bricks(moved, whole_bricks, power)
    previous = shifted_2(moved, "ybrick", 1)
    stacked = jnp.concatenate([previous, moved], axis=1).astype(jnp.float32)
    deskewed = jax.vmap(deskew_brick, in_axes=(0, 0, 0, None))(stacked, rests, fractions, brick)
    observed = deskewed.astype(jnp.float32) + background
    kernel_y = psf_y / jnp.sum(psf_y)
    kernel_x = psf_x / jnp.sum(psf_x)
    x_forward = band_matrix(kernel_x, 384, 128, RADIUS - 128)
    x_back = band_matrix(kernel_x[::-1], 384, 128, RADIUS - 128)
    y_back = band_matrix(kernel_y[::-1], brick + 2 * RADIUS, brick, 0)
    estimate = observed
    y_forward = band_matrix(kernel_y, brick + 2 * RADIUS, brick, 0)
    for turn_index in range(ITERS):
        extended = with_halo(estimate.astype(jnp.bfloat16), (("ybrick", 1),), RADIUS).astype(
            estimate.dtype
        )
        blurred = along_columns(along_rows(extended, y_forward), x_forward)
        ratio = observed / blurred
        ratio_wide = with_halo(ratio.astype(jnp.bfloat16), (("ybrick", 1),), RADIUS).astype(
            ratio.dtype
        )
        estimate = estimate * along_rows(along_columns(ratio_wide, x_back), y_back)
    return estimate


def solution(mesh):
    return jax.shard_map(
        local,
        mesh=mesh,
        in_specs=(P(None, "ybrick", "scan"), P(), P(), P(), P()),
        out_specs=P("scan", "ybrick", None),
        check_vma=False,
    )
```

profile of v0, /device:TPU:110, one launch (start us, length us, event | category | flops | bytes accessed | tf_op | source)
XLA Modules:
  0.0 653.1 jit_solution(12377713951403409570)
XLA Ops:
  0.0 28.1 %all_to_all.18 = bf16[16,128,512]{2,1,0:T(8,128)(2,1)S(1)} all-to-all(bf16[16,128,512]{2,1,0:T(8,128)(2,1)} %param.13), channel_id=1, replica_groups=mesh['scan'=4,'ybrick'=32] {'scan'}, dimensions={0} | all-to-all | bytes 4194304 | tf_op jit(solution)/shard_map/all_to_all | solution.py:72
  37.5 46.2 %collective-permute-done = bf16[4,128,2048]{2,1,0:T(8,128)(2,1)} collective-permute-done((bf16[4,128,2048]{2,1,0:T(8,128)(2,1)S(1)}, bf16[4,128,2048]{2,1,0:T(8,128)(2,1)}, u32[]{:S(2)}, u32[]{:S(2)}) %collective-permute-start) | collective-permute-done | bytes 2097184 | tf_op jit(solution)/shard_map/ppermute | solution.py:17
  90.0 45.6 %collective-permute-done.1 = bf16[4,128,2048]{2,1,0:T(8,128)(2,1)S(1)} collective-permute-done((bf16[4,128,2048]{2,1,0:T(8,128)(2,1)S(1)}, bf16[4,128,2048]{2,1,0:T(8,128)(2,1)S(1)}, u32[]{:S(2)}, u32[]{:S(2)}) %collective-permute-start.1) | collective-permute-done | bytes 2097184 | tf_op jit(solution)/shard_map/ppermute | solution.py:17
  141.9 41.7 %collective-permute-done.2 = bf16[4,128,2048]{2,1,0:T(8,128)(2,1)} collective-permute-done((bf16[4,128,2048]{2,1,0:T(8,128)(2,1)S(1)}, bf16[4,128,2048]{2,1,0:T(8,128)(2,1)}, u32[]{:S(2)}, u32[]{:S(2)}) %collective-permute-start.2) | collective-permute-done | bytes 2097184 | tf_op jit(solution)/shard_map/ppermute | solution.py:17
  186.8 17.3 %collective-permute-start.3 = (bf16[4,128,2048]{2,1,0:T(8,128)(2,1)}, bf16[4,128,2048]{2,1,0:T(8,128)(2,1)S(1)}, u32[]{:S(2)}, u32[]{:S(2)}) collective-permute-start(bf16[4,128,2048]{2,1,0:T(8,128)(2,1)} %broadcast_select_fusion.2), channel_id=1, source_target_pairs={{0,1},{1,2},{2,3},{3,4},{4,5},{5,6},{6,7},{7,8},{8,9},{9,10},{10,1... | collective-permute-start | bytes 6291464 | tf_op jit(solution)/shard_map/ppermute | solution.py:17
  207.7 7.5 %fusion.34 = f32[1,384,128]{2,0,1:T(1,128)S(1)} fusion(pred[384,128,65]{1,0,2:T(32,128)(4,1)S(1)} %iota_compare_fusion, f32[65]{0:T(128)S(1)} %copy-done.7, f32[]{:T(128)} %reduce_sum.19), kind=kOutput, calls=%fused_computation.47 | convolution fusion | flops 38338624 | bytes 3391752 | tf_op jit(solution)/shard_map/dot_general | solution.py:37
  215.5 30.9 %collective-permute-done.3 = bf16[4,128,2048]{2,1,0:T(8,128)(2,1)S(1)} collective-permute-done((bf16[4,128,2048]{2,1,0:T(8,128)(2,1)}, bf16[4,128,2048]{2,1,0:T(8,128)(2,1)S(1)}, u32[]{:S(2)}, u32[]{:S(2)}) %collective-permute-start.3) | collective-permute-done | bytes 2097184 | tf_op jit(solution)/shard_map/ppermute | solution.py:17
  246.3 5.7 maximum_convert_fusion
  254.6 16.5 %while.54 = (s32[]{:T(128)}, f32[4,256,2048]{2,1,0:T(8,128)}, s32[4,3]{1,0:T(4,128)S(1)}, f32[4,128,2048]{2,1,0:T(8,128)}, s32[]{:T(128)}) while((s32[]{:T(128)}, f32[4,256,2048]{2,1,0:T(8,128)}, s32[4,3]{1,0:T(4,128)S(1)}, f32[4,128,2048]{2,1,0:T(8,128)}, s32[]{:T(128)}) %tuple.163), condition=%wide.while_cond, body=%wide.while_body.sunk | while | flops 2 | bytes 2098793 | solution.py:66
  273.6 16.9 %while.55 = (s32[]{:T(128)}, f32[4,256,2048]{2,1,0:T(8,128)}, s32[4,3]{1,0:T(4,128)S(1)}, f32[4,128,2048]{2,1,0:T(8,128)}, s32[]{:T(128)}) while((s32[]{:T(128)}, f32[4,256,2048]{2,1,0:T(8,128)}, s32[4,3]{1,0:T(4,128)S(1)}, f32[4,128,2048]{2,1,0:T(8,128)}, s32[]{:T(128)}) %tuple.178), condition=%wide.while_cond.1, body=%wide.while_body.1.sunk | while | flops 2 | bytes 2098793 | solution.py:67
  290.5 6.0 fusion.40
  296.6 10.0 %collective-permute-start.4 = (bf16[4,32,2048]{2,1,0:T(8,128)(2,1)S(1)}, bf16[4,32,2048]{2,1,0:T(8,128)(2,1)S(1)}, u32[]{:S(2)}, u32[]{:S(2)}) collective-permute-start(bf16[4,32,2048]{2,1,0:T(8,128)(2,1)S(1)} %get-tuple-element.379), channel_id=1, source_target_pairs={{0,1},{1,2},{2,3},{3,4},{4,5},{5,6},{6,7},{7,8},{8,9},{9,10},{10,1... | collective-permute-start | bytes 1572872 | tf_op jit(solution)/shard_map/ppermute | solution.py:27
  314.3 9.8 %collective-permute-done.5 = bf16[4,32,2048]{2,1,0:T(8,128)(2,1)S(1)} collective-permute-done((bf16[4,32,2048]{2,1,0:T(8,128)(2,1)S(1)}, bf16[4,32,2048]{2,1,0:T(8,128)(2,1)S(1)}, u32[]{:S(2)}, u32[]{:S(2)}) %collective-permute-start.5) | collective-permute-done | bytes 524320 | tf_op jit(solution)/shard_map/ppermute | solution.py:28
  324.2 6.0 convolution_bitcast_fusion.1
  332.7 56.8 %while.50 = (s32[]{:T(128)}, f32[4,128,2048]{2,1,0:T(8,128)}, f32[4,128,2048]{1,2,0:T(8,128)}, f32[384,128]{0,1:T(8,128)S(1)}, s32[]{:T(128)}, /*index=5*/f32[]{:T(128)}) while((s32[]{:T(128)}, f32[4,128,2048]{2,1,0:T(8,128)}, f32[4,128,2048]{1,2,0:T(8,128)}, f32[384,128]{0,1:T(8,128)S(1)}, s32[]{:T(128)}, /*index=5*/f32[]{:T(128)}) %tuple.179), condition=%wide.region_3.4_spmd, body=%wide.region_2.3_spmd.sunk | while | flops 1209532416 | bytes 25494092 | solution.py:55
  338.7 5.6 fusion.110
  352.9 5.6 fusion.110
  367.1 5.6 fusion.110
  381.3 5.6 fusion.110
  404.8 12.0 %fusion.32 = f32[1,384,128]{2,0,1:T(1,128)S(1)} fusion(pred[384,128,65]{1,0,2:T(32,128)(4,1)} %copy-done, f32[65]{0:T(128)S(1)} %reverse.6, f32[]{:T(128)} %reduce_sum.19), kind=kOutput, calls=%fused_computation.45 | convolution fusion | flops 38338624 | bytes 3391752 | tf_op jit(solution)/shard_map/dot_general | solution.py:37
  423.7 41.8 %while.51 = (s32[]{:T(128)}, f32[4,192,2048]{2,1,0:T(8,128)}, f32[4,192,2048]{2,1,0:T(8,128)}, f32[384,128]{1,0:T(8,128)S(1)}, s32[]{:T(128)}, /*index=5*/f32[]{:T(128)}) while((s32[]{:T(128)}, f32[4,192,2048]{2,1,0:T(8,128)}, f32[4,192,2048]{2,1,0:T(8,128)}, f32[384,128]{1,0:T(8,128)S(1)}, s32[]{:T(128)}, /*index=5*/f32[]{:T(128)}) %tuple.181), condition=%wide.region_5.6_spmd, body=%wide.region_4.5_spmd.sunk | while | flops 1814298624 | bytes 32244300 | solution.py:55
  465.5 11.8 %fusion.82 = (bf16[4,128,2048]{2,1,0:T(8,128)(2,1)S(1)}, f32[4,128,2048]{2,1,0:T(8,128)}) fusion(f32[4,192,2048]{2,1,0:T(8,128)} %get-tuple-element.218, f32[192,128,1]{1,0,2:T(8,128)} %bitcast.111, bf16[4,128,2048]{2,1,0:T(8,128)(2,1)} %get-tuple-element.350), kind=kOutput, calls=%fused_computation.139 | convolution fusion | flops 2420113408 | bytes 14778368 | tf_op jit(solution)/shard_map/io,pix->pox/dot_general | solution.py:41
  477.4 7.6 %collective-permute-start.8 = (bf16[4,32,2048]{2,1,0:T(8,128)(2,1)S(1)}, bf16[4,32,2048]{2,1,0:T(8,128)(2,1)}, u32[]{:S(2)}, u32[]{:S(2)}) collective-permute-start(bf16[4,32,2048]{2,1,0:T(8,128)(2,1)S(1)} %get-tuple-element.375), channel_id=1, source_target_pairs={{0,1},{1,2},{2,3},{3,4},{4,5},{5,6},{6,7},{7,8},{8,9},{9,10},{10,1... | collective-permute-start | bytes 1572872 | tf_op jit(solution)/shard_map/ppermute | solution.py:27
  491.7 10.2 %collective-permute-done.9 = bf16[4,32,2048]{2,1,0:T(8,128)(2,1)} collective-permute-done((bf16[4,32,2048]{2,1,0:T(8,128)(2,1)S(1)}, bf16[4,32,2048]{2,1,0:T(8,128)(2,1)}, u32[]{:S(2)}, u32[]{:S(2)}) %collective-permute-start.9) | collective-permute-done | bytes 524320 | tf_op jit(solution)/shard_map/ppermute | solution.py:28
  502.0 7.7 %convolution_bitcast_fusion = f32[4,128,2048]{1,2,0:T(8,128)} fusion(f32[192,128,1]{1,0,2:T(8,128)} %bitcast.114, bf16[4,32,2048]{2,1,0:T(8,128)(2,1)} %collective-permute-done.9, bf16[4,128,2048]{2,1,0:T(8,128)(2,1)S(1)} %get-tuple-element.385, bf16[4,32,2048]{2,1,0:T(8,128)(2,1)} %collective-permute-done.8), kind=kOutput, calls=%fused_computation.62 | convolution fusion | flops 2425356288 | bytes 7438336 | tf_op jit(solution)/shard_map/io,pix->pox/dot_general | solution.py:41
  512.2 57.0 %while.52 = (s32[]{:T(128)}, f32[4,128,2048]{2,1,0:T(8,128)}, f32[4,128,2048]{1,2,0:T(8,128)}, f32[384,128]{0,1:T(8,128)S(1)}, s32[]{:T(128)}, /*index=5*/f32[]{:T(128)}) while((s32[]{:T(128)}, f32[4,128,2048]{2,1,0:T(8,128)}, f32[4,128,2048]{1,2,0:T(8,128)}, f32[384,128]{0,1:T(8,128)S(1)}, s32[]{:T(128)}, /*index=5*/f32[]{:T(128)}) %tuple.180), condition=%wide.region_7.8_spmd, body=%wide.region_6.7_spmd.sunk | while | flops 1209532416 | bytes 25494092 | solution.py:55
  518.2 5.6 fusion.118
  532.5 5.6 fusion.118
  546.7 5.6 fusion.118
  584.0 7.7 %collective-permute-done.11 = bf16[4,32,2048]{2,1,0:T(8,128)(2,1)S(1)} collective-permute-done((bf16[4,32,2048]{2,1,0:T(8,128)(2,1)S(1)}, bf16[4,32,2048]{2,1,0:T(8,128)(2,1)S(1)}, u32[]{:S(2)}, u32[]{:S(2)}) %collective-permute-start.11) | collective-permute-done | bytes 524320 | tf_op jit(solution)/shard_map/ppermute | solution.py:28
  598.5 41.9 %while.53 = (s32[]{:T(128)}, f32[4,192,2048]{2,1,0:T(8,128)}, f32[4,192,2048]{2,1,0:T(8,128)}, f32[384,128]{1,0:T(8,128)S(1)}, s32[]{:T(128)}, /*index=5*/f32[]{:T(128)}) while((s32[]{:T(128)}, f32[4,192,2048]{2,1,0:T(8,128)}, f32[4,192,2048]{2,1,0:T(8,128)}, f32[384,128]{1,0:T(8,128)S(1)}, s32[]{:T(128)}, /*index=5*/f32[]{:T(128)}) %tuple.182), condition=%wide.region_9.10_spmd, body=%wide.region_8.9_spmd.sunk | while | flops 1814298624 | bytes 32244300 | solution.py:55
  640.3 12.5 %bitcast_multiply_fusion = f32[4,128,2048]{2,1,0:T(8,128)} fusion(f32[4,128,2048]{2,1,0:T(8,128)} %get-tuple-element.386, f32[4,192,2048]{2,1,0:T(8,128)} %get-tuple-element.220, f32[192,128,1]{1,0,2:T(8,128)S(1)} %bitcast.112), kind=kOutput, calls=%fused_computation.55 | convolution fusion | flops 2416967680 | bytes 14778368 | tf_op jit(solution)/shard_map/io,pix->pox/dot_general | solution.py:41
  (216 shorter events, 288.1 us)
Async XLA Ops:
  28.1 9.3 %copy-start.4 = (s32[16]{0:T(128)S(1)}, s32[16]{0:T(128)}, u32[]{:S(2)}) copy-start(s32[16]{0:T(128)} %param.14) | copy-start | bytes 196
  34.3 49.4 %collective-permute-start = (bf16[4,128,2048]{2,1,0:T(8,128)(2,1)S(1)}, bf16[4,128,2048]{2,1,0:T(8,128)(2,1)}, u32[]{:S(2)}, u32[]{:S(2)}) collective-permute-start(bf16[4,128,2048]{2,1,0:T(8,128)(2,1)S(1)} %all_to_all.16), channel_id=1, source_target_pairs={{0,1},{1,2},{2,3},{3,4},{4,5},{5,6},{6,7},{7,8},{8,9},{9,10},{10,1... | collective-permute-start | bytes 6291464 | tf_op jit(solution)/shard_map/ppermute | solution.py:17
  85.6 54.9 %copy-start.6 = (f32[65]{0:T(128)S(1)}, f32[65]{0:T(128)}, u32[]{:S(2)}) copy-start(f32[65]{0:T(128)} %param.16) | copy-start | bytes 784
  85.6 55.7 %copy-start.7 = (f32[65]{0:T(128)S(1)}, f32[65]{0:T(128)}, u32[]{:S(2)}) copy-start(f32[65]{0:T(128)} %param.17) | copy-start | bytes 784
  85.6 50.0 %collective-permute-start.1 = (bf16[4,128,2048]{2,1,0:T(8,128)(2,1)S(1)}, bf16[4,128,2048]{2,1,0:T(8,128)(2,1)S(1)}, u32[]{:S(2)}, u32[]{:S(2)}) collective-permute-start(bf16[4,128,2048]{2,1,0:T(8,128)(2,1)S(1)} %broadcast_select_fusion), channel_id=1, source_target_pairs={{0,2},{1,3},{2,4},{3,5},{4,6},{5,7},{6,8},{7,9},{8,10},{9,11},{10,... | collective-permute-start | bytes 6291464 | tf_op jit(solution)/shard_map/ppermute | solution.py:17
  135.8 47.7 %collective-permute-start.2 = (bf16[4,128,2048]{2,1,0:T(8,128)(2,1)S(1)}, bf16[4,128,2048]{2,1,0:T(8,128)(2,1)}, u32[]{:S(2)}, u32[]{:S(2)}) collective-permute-start(bf16[4,128,2048]{2,1,0:T(8,128)(2,1)S(1)} %broadcast_select_fusion.1), channel_id=1, source_target_pairs={{0,4},{1,5},{2,6},{3,7},{4,8},{5,9},{6,10},{7,11},{8,12},{9,13},{1... | collective-permute-start | bytes 6291464 | tf_op jit(solution)/shard_map/ppermute | solution.py:17
  186.8 59.6 %collective-permute-start.3 = (bf16[4,128,2048]{2,1,0:T(8,128)(2,1)}, bf16[4,128,2048]{2,1,0:T(8,128)(2,1)S(1)}, u32[]{:S(2)}, u32[]{:S(2)}) collective-permute-start(bf16[4,128,2048]{2,1,0:T(8,128)(2,1)} %broadcast_select_fusion.2), channel_id=1, source_target_pairs={{0,1},{1,2},{2,3},{3,4},{4,5},{5,6},{6,7},{7,8},{8,9},{9,10},{10,1... | collective-permute-start | bytes 6291464 | tf_op jit(solution)/shard_map/ppermute | solution.py:17
  206.0 1.7 copy-start
  207.7 7.7 %copy-start.5 = (s32[16]{0:T(128)S(1)}, s32[16]{0:T(128)}, u32[]{:S(2)}) copy-start(s32[16]{0:T(128)} %param.15) | copy-start | bytes 196
  296.6 17.8 %collective-permute-start.4 = (bf16[4,32,2048]{2,1,0:T(8,128)(2,1)S(1)}, bf16[4,32,2048]{2,1,0:T(8,128)(2,1)S(1)}, u32[]{:S(2)}, u32[]{:S(2)}) collective-permute-start(bf16[4,32,2048]{2,1,0:T(8,128)(2,1)S(1)} %get-tuple-element.379), channel_id=1, source_target_pairs={{0,1},{1,2},{2,3},{3,4},{4,5},{5,6},{6,7},{7,8},{8,9},{9,10},{10,1... | collective-permute-start | bytes 1572872 | tf_op jit(solution)/shard_map/ppermute | solution.py:27
  306.6 17.6 %collective-permute-start.5 = (bf16[4,32,2048]{2,1,0:T(8,128)(2,1)S(1)}, bf16[4,32,2048]{2,1,0:T(8,128)(2,1)S(1)}, u32[]{:S(2)}, u32[]{:S(2)}) collective-permute-start(bf16[4,32,2048]{2,1,0:T(8,128)(2,1)S(1)} %get-tuple-element.380), channel_id=1, source_target_pairs={{1,0},{2,1},{3,2},{4,3},{5,4},{6,5},{7,6},{8,7},{9,8},{10,9},{11,1... | collective-permute-start | bytes 1572872 | tf_op jit(solution)/shard_map/ppermute | solution.py:28
  309.5 1.2 copy-start.1
  314.2 16.0 %copy-start.8 = (f32[1,192,128]{2,0,1:T(1,128)}, f32[1,192,128]{2,0,1:T(1,128)S(1)}, u32[]{:S(2)}) copy-start(f32[1,192,128]{2,0,1:T(1,128)S(1)} %fusion.38) | copy-start | bytes 294916
  389.5 11.0 %copy-start.2 = (pred[192,128,65]{1,0,2:T(32,128)(4,1)S(1)}, pred[192,128,65]{1,0,2:T(32,128)(4,1)}, u32[]{:S(2)}) copy-start(pred[192,128,65]{1,0,2:T(32,128)(4,1)} %copy-done.1) | copy-start | bytes 4792324
  394.3 22.5 %collective-permute-start.6 = (bf16[4,32,2048]{2,1,0:T(8,128)(2,1)}, bf16[4,32,2048]{2,1,0:T(8,128)(2,1)S(1)}, u32[]{:S(2)}, u32[]{:S(2)}) collective-permute-start(bf16[4,32,2048]{2,1,0:T(8,128)(2,1)} %get-tuple-element.377), channel_id=1, source_target_pairs={{0,1},{1,2},{2,3},{3,4},{4,5},{5,6},{6,7},{7,8},{8,9},{9,10},{10,1... | collective-permute-start | bytes 1572872 | tf_op jit(solution)/shard_map/ppermute | solution.py:27
  396.2 20.6 %collective-permute-start.7 = (bf16[4,32,2048]{2,1,0:T(8,128)(2,1)}, bf16[4,32,2048]{2,1,0:T(8,128)(2,1)S(1)}, u32[]{:S(2)}, u32[]{:S(2)}) collective-permute-start(bf16[4,32,2048]{2,1,0:T(8,128)(2,1)} %get-tuple-element.378), channel_id=1, source_target_pairs={{1,0},{2,1},{3,2},{4,3},{5,4},{6,5},{7,6},{8,7},{9,8},{10,9},{11,1... | collective-permute-start | bytes 1572872 | tf_op jit(solution)/shard_map/ppermute | solution.py:28
  477.4 14.3 %collective-permute-start.8 = (bf16[4,32,2048]{2,1,0:T(8,128)(2,1)S(1)}, bf16[4,32,2048]{2,1,0:T(8,128)(2,1)}, u32[]{:S(2)}, u32[]{:S(2)}) collective-permute-start(bf16[4,32,2048]{2,1,0:T(8,128)(2,1)S(1)} %get-tuple-element.375), channel_id=1, source_target_pairs={{0,1},{1,2},{2,3},{3,4},{4,5},{5,6},{6,7},{7,8},{8,9},{9,10},{10,1... | collective-permute-start | bytes 1572872 | tf_op jit(solution)/shard_map/ppermute | solution.py:27
  485.1 16.9 %collective-permute-start.9 = (bf16[4,32,2048]{2,1,0:T(8,128)(2,1)S(1)}, bf16[4,32,2048]{2,1,0:T(8,128)(2,1)}, u32[]{:S(2)}, u32[]{:S(2)}) collective-permute-start(bf16[4,32,2048]{2,1,0:T(8,128)(2,1)S(1)} %get-tuple-element.376), channel_id=1, source_target_pairs={{1,0},{2,1},{3,2},{4,3},{5,4},{6,5},{7,6},{8,7},{9,8},{10,9},{11,1... | collective-permute-start | bytes 1572872 | tf_op jit(solution)/shard_map/ppermute | solution.py:28
  572.9 11.1 %collective-permute-start.10 = (bf16[4,32,2048]{2,1,0:T(8,128)(2,1)S(1)}, bf16[4,32,2048]{2,1,0:T(8,128)(2,1)S(1)}, u32[]{:S(2)}, u32[]{:S(2)}) collective-permute-start(bf16[4,32,2048]{2,1,0:T(8,128)(2,1)S(1)} %get-tuple-element.373), channel_id=1, source_target_pairs={{0,1},{1,2},{2,3},{3,4},{4,5},{5,6},{6,7},{7,8},{8,9},{9,10},{10,1... | collective-permute-start | bytes 1572872 | tf_op jit(solution)/shard_map/ppermute | solution.py:27
  574.8 16.8 %collective-permute-start.11 = (bf16[4,32,2048]{2,1,0:T(8,128)(2,1)S(1)}, bf16[4,32,2048]{2,1,0:T(8,128)(2,1)S(1)}, u32[]{:S(2)}, u32[]{:S(2)}) collective-permute-start(bf16[4,32,2048]{2,1,0:T(8,128)(2,1)S(1)} %get-tuple-element.374), channel_id=1, source_target_pairs={{1,0},{2,1},{3,2},{4,3},{5,4},{6,5},{7,6},{8,7},{9,8},{10,9},{11,1... | collective-permute-start | bytes 1572872 | tf_op jit(solution)/shard_map/ppermute | solution.py:28
  598.5 41.9 %copy-start.3 = (f32[1,192,128]{2,0,1:T(1,128)S(1)}, f32[1,192,128]{2,0,1:T(1,128)}, u32[]{:S(2)}) copy-start(f32[1,192,128]{2,0,1:T(1,128)} %fusion.36) | copy-start | bytes 294916
where the time goes:
time: 659 us; the launch traced here: 653 us
  waiting for transfers between devices  202 us (31%)
  local copies, waits for them, and re-layouts  181 us (27%)
  matrix products  142 us (22%)
  starting transfers between devices  63 us (10%)
  other arithmetic  35.6 us (5%)
  blocking collectives  28.1 us (4%)
    ppermute x4, waiting for transfers between devices, shifted_2(): return lax.ppermute(x, axis, pairs)  164 us
    dot_general x16, matrix products, per_frame(): jnp.einsum('rbi,io->rbo', windows, matrix, precision=lax.Precision.HIGHEST)  77 us
    dot_general x4, matrix products, along_rows(): jnp.einsum('io,pix->pox', matrix, source, precision=lax.Precision.HIGHEST)  38 us
    gather x24, local copies, waits for them, and re-layouts  33.4 us
    dynamic_update_slice x24, local copies, waits for them, and re-layouts, along_columns(): return lax.map(per_frame, source)  31.3 us
    ppermute x4, starting transfers between devices, shifted_2(): return lax.ppermute(x, axis, pairs)  29.2 us
    all_to_all x1, blocking collectives, local(): lax.all_to_all(raw, 'scan', split_axis=0, concat_axis=2, tiled=True)  28.1 us
    ppermute x4, waiting for transfers between devices, with_halo(): after = lax.ppermute(initial, axis, down)  27.7 us
  transfers between devices with their start and end apart: 12, of which 10 were waited for; matrix products, arithmetic and copies ran while one was open for 5% of the time, Pallas kernels for 0%

commit v1 on v0

v1 whole, which is shorter than its diff:
```python
import functools

import jax
import jax.numpy as jnp
from jax import lax
from jax.experimental import pallas as pl
from jax.experimental.pallas import tpu as pltpu
from jax.sharding import PartitionSpec as P

RADIUS = 32
TAPS = 2 * RADIUS + 1
ITERS = 2
NFRAC = 16
BRICK = 128
BRICKS = 32
COLS = 512
HALO = 2 * ITERS * RADIUS
REACH = 8
HALF = 16
WINDOW = HALF + 1
SLOTS = WINDOW + REACH
ROWS = WINDOW * BRICK
WIDE = COLS + 2 * HALO
STEP = 192
SPAN = STEP + 2 * RADIUS
BLOCK = 2 * STEP
PADDED = 6 * BLOCK
TINY = 1e-30

background = 0.5


def toeplitz(kernel, count_out, count_in):
    padded = jnp.pad(kernel, (0, count_in + 1 - TAPS))
    return jnp.tile(padded, count_out)[: count_out * count_in].reshape(count_out, count_in)


def rows_band(kernel):
    return toeplitz(kernel, STEP, SPAN).astype(jnp.bfloat16)


def columns_band(kernel):
    band = toeplitz(kernel, 256, 416)
    return jnp.pad(band, ((0, 0), (96, 0))).T.astype(jnp.bfloat16)


def deskew_kernel(scalars, raw_ref, out_ref, buffer):
    half, shift = scalars[0], scalars[1]
    weight = scalars[2].astype(jnp.float32) / NFRAC

    def widen(k, carry):
        brick = k - REACH + (HALF - 1) * half
        tile = raw_ref[jnp.maximum(brick, 0)].astype(jnp.float32)
        buffer[pl.ds(pl.multiple_of(k * BRICK, BRICK), BRICK), :] = jnp.where(brick >= 0, tile, 0.0)
        return carry

    lax.fori_loop(0, SLOTS, widen, 0)

    def blend(i, carry):
        start = REACH * BRICK + BRICK * i - shift - 1
        rest = lax.rem(start, 8)
        tall = BRICK + 16
        rows = buffer[pl.ds(pl.multiple_of(start - rest, 8), tall), :]
        lower = pltpu.roll(rows, lax.rem(tall - rest, tall), 0)[:BRICK]
        upper = pltpu.roll(rows, tall - 1 - rest, 0)[:BRICK]
        mixed = (1.0 - weight) * upper + weight * lower
        out_ref[pl.ds(pl.multiple_of(i * BRICK, BRICK), BRICK), :] = mixed.astype(jnp.bfloat16)
        return carry

    lax.fori_loop(0, WINDOW, blend, 0)


def filter_kernel(
    scalars, left, middle, right, y_forward, y_back, x_forward, x_back, out_ref, observed, estimate, rounded, back, rows_done, ratio
):
    half, scan = scalars[0], scalars[1]
    zeros = jnp.zeros((RADIUS, WIDE), jnp.bfloat16)
    for ref in (rounded, back):
        ref[pl.ds(0, RADIUS), :] = zeros
        ref[pl.ds(RADIUS + PADDED, RADIUS), :] = zeros
    tail = PADDED - ROWS
    observed[pl.ds(ROWS, tail), :] = jnp.zeros((tail, WIDE), jnp.float32)
    rounded[pl.ds(RADIUS + ROWS, tail), :] = jnp.zeros((tail, WIDE), jnp.bfloat16)

    def load(i, carry):
        rows = pl.ds(pl.multiple_of(i * BRICK, BRICK), BRICK)
        target = pl.ds(pl.multiple_of(i * BRICK + RADIUS, RADIUS), BRICK)
        for ref, first, width, inside in (
            (left, 0, HALO, scan > 0),
            (middle, HALO, COLS, None),
            (right, HALO + COLS, HALO, scan < 3),
        ):
            values = ref[rows, :].astype(jnp.float32) + background
            if inside is not None:
                values = jnp.where(inside, values, 0.0)
            observed[rows, pl.ds(first, width)] = values
            rounded[target, pl.ds(first, width)] = values.astype(jnp.bfloat16)
        return carry

    lax.fori_loop(0, WINDOW, load, 0)

    windows = ((0, 384, 128), (128, 640, 0), (384, 768, 0))

    def columns(source, band, block):
        low, high, offset = windows[block]
        return jnp.dot(
            source[:, low:high], band[offset : offset + high - low, :], preferred_element_type=jnp.float32
        )

    def forward(i, carry):
        base = i * BLOCK
        for q in range(2):
            window = rounded[pl.ds(pl.multiple_of(base + q * STEP, 64), SPAN), :]
            rows_done[pl.ds(q * STEP, STEP), :] = jnp.dot(
                y_forward[...], window, preferred_element_type=jnp.float32
            ).astype(jnp.bfloat16)
        rows = pl.ds(pl.multiple_of(base, BLOCK), BLOCK)
        for block in range(3):
            blurred = columns(rows_done, x_forward, block)
            seen = observed[rows, pl.ds(block * 256, 256)]
            ratio[:, pl.ds(block * 256, 256)] = (seen / jnp.maximum(blurred, TINY)).astype(jnp.bfloat16)
        target = pl.ds(pl.multiple_of(base + RADIUS, RADIUS), BLOCK)
        for block in range(3):
            back[target, pl.ds(block * 256, 256)] = columns(ratio, x_back, block).astype(jnp.bfloat16)
        return carry

    def update(i, carry):
        base = pl.multiple_of(i * STEP, STEP)
        correction = jnp.dot(y_back[...], back[pl.ds(base, SPAN), :], preferred_element_type=jnp.float32)
        fresh = observed[pl.ds(base, STEP), :] * correction
        estimate[pl.ds(base, STEP), :] = fresh
        rounded[pl.ds(pl.multiple_of(base + RADIUS, RADIUS), STEP), :] = fresh.astype(jnp.bfloat16)
        return carry

    def finish(i, carry):
        base = jnp.minimum(i * STEP, HALF * BRICK - STEP)
        source = pl.multiple_of(base + BRICK * half, 64)
        correction = jnp.dot(
            y_back[...], back[pl.ds(source, SPAN), pl.ds(HALO, COLS)], preferred_element_type=jnp.float32
        )
        final = estimate[pl.ds(source, STEP), pl.ds(HALO, COLS)] * correction
        out_ref[pl.ds(pl.multiple_of(base, 64), STEP), :] = (final * final).astype(jnp.bfloat16)
        return carry

    lax.fori_loop(0, PADDED // BLOCK, forward, 0)
    lax.fori_loop(0, PADDED // STEP, update, 0)
    lax.fori_loop(0, PADDED // BLOCK, forward, 0)
    lax.fori_loop(0, -(-HALF * BRICK // STEP), finish, 0)


SMEM = pl.BlockSpec(memory_space=pltpu.SMEM)
VMEM = pl.BlockSpec(memory_space=pltpu.VMEM)


def deskew(half, shift, fraction, raw):
    return pl.pallas_call(
        deskew_kernel,
        out_shape=jax.ShapeDtypeStruct((ROWS, COLS), jnp.bfloat16),
        in_specs=[SMEM, VMEM],
        out_specs=VMEM,
        scratch_shapes=[pltpu.VMEM((SLOTS * BRICK + 16, COLS), jnp.float32)],
        compiler_params=pltpu.CompilerParams(vmem_limit_bytes=60 * 2**20),
    )(jnp.stack([half, shift, fraction]), raw)


def deconvolve(half, scan, left, middle, right, kernel_y, kernel_x):
    return pl.pallas_call(
        filter_kernel,
        out_shape=jax.ShapeDtypeStruct((HALF * BRICK, COLS), jnp.bfloat16),
        in_specs=[SMEM] + [VMEM] * 7,
        out_specs=VMEM,
        scratch_shapes=[
            pltpu.VMEM((PADDED, WIDE), jnp.float32),
            pltpu.VMEM((PADDED, WIDE), jnp.float32),
            pltpu.VMEM((PADDED + 2 * RADIUS, WIDE), jnp.bfloat16),
            pltpu.VMEM((PADDED + 2 * RADIUS, WIDE), jnp.bfloat16),
            pltpu.VMEM((BLOCK, WIDE), jnp.bfloat16),
            pltpu.VMEM((BLOCK, WIDE), jnp.bfloat16),
        ],
        compiler_params=pltpu.CompilerParams(vmem_limit_bytes=60 * 2**20),
    )(
        jnp.stack([half, scan]),
        left,
        middle,
        right,
        rows_band(kernel_y),
        rows_band(kernel_y[::-1]),
        columns_band(kernel_x),
        columns_band(kernel_x[::-1]),
    )


def local(raw, row_shift, frac_index, psf_y, psf_x):
    scan = lax.axis_index("scan").astype(jnp.int32)
    spot = lax.axis_index("ybrick").astype(jnp.int32)
    half, plane = spot // HALF, spot % HALF
    gathered = lax.all_to_all(jnp.concatenate([raw, raw], axis=0), "ybrick", split_axis=0, concat_axis=0, tiled=True)
    shift = lax.dynamic_index_in_dim(row_shift, plane, keepdims=False)
    fraction = lax.dynamic_index_in_dim(frac_index, plane, keepdims=False)
    middle = deskew(half, shift, fraction, gathered)
    left = lax.ppermute(middle[:, COLS - HALO :], "scan", [(i, i + 1) for i in range(3)])
    right = lax.ppermute(middle[:, :HALO], "scan", [(i + 1, i) for i in range(3)])
    kernel_y = psf_y / jnp.sum(psf_y)
    kernel_x = psf_x / jnp.sum(psf_x)
    coded = deconvolve(half, scan, left, middle, right, kernel_y, kernel_x).reshape(HALF, BRICK, COLS)
    groups = [list(range(HALF)), list(range(HALF, 2 * HALF))]
    coded = lax.all_to_all(coded, "ybrick", split_axis=0, concat_axis=0, axis_index_groups=groups, tiled=True)
    coded = lax.all_to_all(coded, "scan", split_axis=0, concat_axis=2, tiled=True)
    return jnp.sqrt(coded.astype(jnp.float32))


def solution(mesh):
    return jax.shard_map(
        local,
        mesh=mesh,
        in_specs=(P(None, "ybrick", "scan"), P(), P(), P(), P()),
        out_specs=P("scan", "ybrick", None),
        check_vma=False,
    )
```

time: 659 us -> 190 us (0.29)
  the two profiles are of different devices: /device:TPU:110 before, /device:TPU:1 now
where the time goes in v1:
time: 190 us
  blocking collectives  56.3 us (30%)
  waiting for transfers between devices  50.3 us (26%)
  Pallas kernels  29.9 us (16%)
  starting transfers between devices  22 us (12%)
  local copies, waits for them, and re-layouts  20 us (11%)
  other arithmetic  10.8 us (6%)
    all_to_all x1, waiting for transfers between devices, local(): lax.all_to_all(jnp.concatenate([raw, raw], axis=0), 'ybrick', split_axis=...  45.7 us
    all_to_all x1, blocking collectives, local(): lax.all_to_all(coded, 'ybrick', split_axis=0, concat_axis=0, axis_index_g...  28.3 us
    all_to_all x1, blocking collectives, local(): lax.all_to_all(coded, 'scan', split_axis=0, concat_axis=2, tiled=True)  28 us
    pallas_call x1, Pallas kernels, deconvolve(): pl.pallas_call(filter_kernel, out_shape=jax.ShapeDtypeStruct((HALF * BRIC...  22 us
    all_to_all x1, starting transfers between devices, local(): lax.all_to_all(jnp.concatenate([raw, raw], axis=0), 'ybrick', split_axis=...  11.6 us
    sqrt x2, local copies, waits for them, and re-layouts, local(): return jnp.sqrt(coded.astype(jnp.float32))  10.7 us
    ppermute x1, starting transfers between devices, local(): lax.ppermute(middle[:, COLS - HALO:], 'scan', [(i, i + 1) for i in range(...  8.52 us
    pallas_call x1, Pallas kernels, deskew(): pl.pallas_call(deskew_kernel, out_shape=jax.ShapeDtypeStruct((ROWS, COLS)...  7.86 us
  transfers between devices with their start and end apart: 3, of which 3 were waited for; matrix products, arithmetic and copies ran while one was open for 7% of the time, Pallas kernels for 0%

profile of v1, /device:TPU:1, one launch (start us, length us, event | category | flops | bytes accessed | tf_op | source)
XLA Modules:
  0.0 189.6 jit_solution(18134302061534782008)
XLA Ops:
  0.0 4.6 %pad_maximum_fusion = bf16[32,128,512]{2,1,0:T(8,128)(2,1)} fusion(bf16[16,128,512]{2,1,0:T(8,128)(2,1)} %param.5), kind=kLoop, calls=%fused_computation | loop fusion | flops 2097152 | bytes 6291456 | tf_op jit(solution)/shard_map/concatenate | solution.py:197
  4.6 11.6 %all-to-all-start = ((bf16[32,128,512]{2,1,0:T(8,128)(2,1)}), bf16[32,128,512]{2,1,0:T(8,128)(2,1)}, u32[]{:S(2)}, u32[]{:S(2)}) async-start(bf16[32,128,512]{2,1,0:T(8,128)(2,1)} %pad_maximum_fusion), calls=%async_computation | async-start | bytes 8388608 | tf_op jit(solution)/shard_map/all_to_all | solution.py:197
  16.3 0.7 reduce_sum.18
  17.1 0.7 reduce_sum.19
  17.8 0.7 dynamic_slice.8
  18.5 0.6 dynamic_slice.7
  19.0 0.7 broadcast_divide_fusion.2
  19.7 0.4 tile.41
  20.1 0.7 convert_element_type.27.y_forward
  20.8 0.4 tile.43
  21.2 0.7 convert_element_type.28.y_back
  21.9 1.9 %pad_add_fusion.1.scalars = s32[3]{0:T(128)} fusion(s32[1]{0:T(128)} %dynamic_slice.8, s32[1]{0:T(128)} %dynamic_slice.7, s32[1]{0:T(128)} %bitcast), kind=kLoop, calls=%fused_computation.10 | loop fusion | flops 6 | bytes 24 | tf_op jit(solution)/shard_map/stack | solution.py:163
  23.8 0.6 broadcast_divide_fusion
  24.4 45.7 %all-to-all-done.raw_ref = bf16[32,128,512]{2,1,0:T(8,128)(2,1)} async-done(((bf16[32,128,512]{2,1,0:T(8,128)(2,1)}), bf16[32,128,512]{2,1,0:T(8,128)(2,1)}, u32[]{:S(2)}, u32[]{:S(2)}) %all-to-all-start) | async-done | bytes 4194336 | tf_op jit(solution)/shard_map/all_to_all | solution.py:197
  70.1 7.9 %shard_map.55.middle = bf16[2176,512]{1,0:T(8,128)(2,1)} custom-call(s32[3]{0:T(128)} %pad_add_fusion.1.scalars, bf16[32,128,512]{2,1,0:T(8,128)(2,1)} %all-to-all-done.raw_ref), custom_call_target="tpu_custom_call" | custom-call | tf_op jit(solution)/shard_map/pallas_call | solution.py:156
  78.0 1.3 fusion
  79.3 8.5 %collective-permute-start = (bf16[2176,128]{1,0:T(8,128)(2,1)S(1)}, bf16[2176,128]{1,0:T(8,128)(2,1)S(1)}, u32[]{:S(2)}, u32[]{:S(2)}) collective-permute-start(bf16[2176,128]{1,0:T(8,128)(2,1)S(1)} %get-tuple-element.6), channel_id=1, source_target_pairs={{0,32},{32,64},{64,96},{1,33},{33,65},{65,97},{2,34},{34,66},{66,9... | collective-permute-start | bytes 1671176 | tf_op jit(solution)/shard_map/ppermute | solution.py:201
  87.8 1.9 %collective-permute-start.1 = (bf16[2176,128]{1,0:T(8,128)(2,1)S(1)}, bf16[2176,128]{1,0:T(8,128)(2,1)S(1)}, u32[]{:S(2)}, u32[]{:S(2)}) collective-permute-start(bf16[2176,128]{1,0:T(8,128)(2,1)S(1)} %get-tuple-element.5), channel_id=1, source_target_pairs={{32,0},{64,32},{96,64},{33,1},{65,33},{97,65},{34,2},{66,34},{98,6... | collective-permute-start | bytes 1671176 | tf_op jit(solution)/shard_map/ppermute | solution.py:202
  89.8 0.6 tile.45
  90.9 0.6 tile.47
  91.5 0.3 reshape.24
  92.0 0.6 pad_add_fusion.scalars
  92.6 0.7 pad_bitcast_fusion.1.x_forward
  93.4 0.7 pad_bitcast_fusion.x_back
  94.3 4.4 %collective-permute-done.1.right = bf16[2176,128]{1,0:T(8,128)(2,1)S(1)} collective-permute-done((bf16[2176,128]{1,0:T(8,128)(2,1)S(1)}, bf16[2176,128]{1,0:T(8,128)(2,1)S(1)}, u32[]{:S(2)}, u32[]{:S(2)}) %collective-permute-start.1) | collective-permute-done | bytes 557088 | tf_op jit(solution)/shard_map/ppermute | solution.py:202
  98.7 0.8 copy-done.1
  99.5 22.0 %shard_map.56 = bf16[2048,512]{1,0:T(8,128)(2,1)} custom-call(s32[2]{0:T(128)} %pad_add_fusion.scalars, bf16[2176,128]{1,0:T(8,128)(2,1)} %copy-done, bf16[2176,512]{1,0:T(8,128)(2,1)} %shard_map.55.middle, bf16[2176,128]{1,0:T(8,128)(2,1)} %copy-done.1, bf16[192,256]{1,0:T(8,128)(2,1)} %convert_element_type.27.y_forward, ...), custom_call_target="tpu_custom_call" | custom-call | tf_op jit(solution)/shard_map/pallas_call | solution.py:167
  121.5 28.3 %all_to_all.19 = bf16[16,128,512]{2,1,0:T(8,128)(2,1)S(1)} all-to-all(bf16[16,128,512]{2,1,0:T(8,128)(2,1)} %bitcast.13), channel_id=1, replica_groups={{0,1,2,3,4,5,6,7,8,9,10,11,12,13,14,15},{16,17,18,19,20,21,22,23,24,25,..., dimensions={0} | all-to-all | bytes 4194304 | tf_op jit(solution)/shard_map/all_to_all | solution.py:207
  149.8 28.0 %all_to_all.20 = bf16[16,128,512]{2,1,0:T(8,128)(2,1)S(1)} all-to-all(bf16[16,128,512]{2,1,0:T(8,128)(2,1)S(1)} %all_to_all.19), channel_id=1, replica_groups=mesh['scan'=4,'ybrick'=32] {'scan'}, dimensions={0} | all-to-all | bytes 4194304 | tf_op jit(solution)/shard_map/all_to_all | solution.py:208
  177.9 1.1 convert_sqrt_fusion
  178.9 4.6 %copy.11 = f32[4,4,128,512]{3,0,2,1:T(4,128)} copy(f32[4,4,128,512]{3,2,1,0:T(8,128)S(1)} %bitcast.11) | data formatting | bytes 8388608 | tf_op jit(solution)/shard_map/sqrt | solution.py:209
  183.6 6.0 %sqrt.15 = f32[4,128,2048]{2,1,0:T(8,128)} reshape(f32[4,128,4,512]{3,2,1,0:T(4,128)} %bitcast.12) | data formatting | bytes 8388608 | tf_op jit(solution)/shard_map/sqrt | solution.py:209
  (29 shorter events, 1.2 us)
Async XLA Ops:
  4.6 11.6 %copy-start.2 = (f32[65]{0:T(128)S(1)}, f32[65]{0:T(128)}, u32[]{:S(2)}) copy-start(f32[65]{0:T(128)} %param.8) | copy-start | bytes 784
  4.6 12.4 %copy-start.3 = (f32[65]{0:T(128)S(1)}, f32[65]{0:T(128)}, u32[]{:S(2)}) copy-start(f32[65]{0:T(128)} %param.9) | copy-start | bytes 784
  4.6 13.2 %copy-start.4 = (s32[16]{0:T(128)S(1)}, s32[16]{0:T(128)}, u32[]{:S(2)}) copy-start(s32[16]{0:T(128)} %param.7) | copy-start | bytes 196
  4.6 13.8 %copy-start.5 = (s32[16]{0:T(128)S(1)}, s32[16]{0:T(128)}, u32[]{:S(2)}) copy-start(s32[16]{0:T(128)} %param.6) | copy-start | bytes 196
  4.6 65.5 %all-to-all-start = ((bf16[32,128,512]{2,1,0:T(8,128)(2,1)}), bf16[32,128,512]{2,1,0:T(8,128)(2,1)}, u32[]{:S(2)}, u32[]{:S(2)}) async-start(bf16[32,128,512]{2,1,0:T(8,128)(2,1)} %pad_maximum_fusion), calls=%async_computation | async-start | bytes 8388608 | tf_op jit(solution)/shard_map/all_to_all | solution.py:197
  79.3 15.0 %collective-permute-start = (bf16[2176,128]{1,0:T(8,128)(2,1)S(1)}, bf16[2176,128]{1,0:T(8,128)(2,1)S(1)}, u32[]{:S(2)}, u32[]{:S(2)}) collective-permute-start(bf16[2176,128]{1,0:T(8,128)(2,1)S(1)} %get-tuple-element.6), channel_id=1, source_target_pairs={{0,32},{32,64},{64,96},{1,33},{33,65},{65,97},{2,34},{34,66},{66,9... | collective-permute-start | bytes 1671176 | tf_op jit(solution)/shard_map/ppermute | solution.py:201
  87.8 10.9 %collective-permute-start.1 = (bf16[2176,128]{1,0:T(8,128)(2,1)S(1)}, bf16[2176,128]{1,0:T(8,128)(2,1)S(1)}, u32[]{:S(2)}, u32[]{:S(2)}) collective-permute-start(bf16[2176,128]{1,0:T(8,128)(2,1)S(1)} %get-tuple-element.5), channel_id=1, source_target_pairs={{32,0},{64,32},{96,64},{33,1},{65,33},{97,65},{34,2},{66,34},{98,6... | collective-permute-start | bytes 1671176 | tf_op jit(solution)/shard_map/ppermute | solution.py:202
  94.3 4.4 %copy-start = (bf16[2176,128]{1,0:T(8,128)(2,1)}, bf16[2176,128]{1,0:T(8,128)(2,1)S(1)}, u32[]{:S(2)}) copy-start(bf16[2176,128]{1,0:T(8,128)(2,1)S(1)} %collective-permute-done.left) | copy-start | bytes 1671172
  98.7 0.8 copy-start.1

commit v2 on v1

--- a/solution.py
+++ b/solution.py
@@ -49,9 +49,8 @@
     weight = scalars[2].astype(jnp.float32) / NFRAC
 
     def widen(k, carry):
-        brick = k - REACH + (HALF - 1) * half
-        tile = raw_ref[jnp.maximum(brick, 0)].astype(jnp.float32)
-        buffer[pl.ds(pl.multiple_of(k * BRICK, BRICK), BRICK), :] = jnp.where(brick >= 0, tile, 0.0)
+        inside = k + (HALF - 1) * half >= REACH
+        buffer[pl.ds(pl.multiple_of(k * BRICK, BRICK), BRICK), :] = jnp.where(inside, raw_ref[k].astype(jnp.float32), 0.0)
         return carry
 
     lax.fori_loop(0, SLOTS, widen, 0)
@@ -146,6 +145,197 @@
     lax.fori_loop(0, PADDED // STEP, update, 0)
     lax.fori_loop(0, PADDED // BLOCK, forward, 0)
     lax.fori_loop(0, -(-HALF * BRICK // STEP), finish, 0)
+
+
+MESH = pl.DeviceIdType.MESH
+REFS = pl.BlockSpec(memory_space=pl.ANY)
+BOTH_FIRST, BOTH_LAST = HALF - 1 - REACH, HALF
+
+
+def slot_of(brick, half):
+    return brick + REACH - (HALF - 1) * half
+
+
+def gather_kernel(raw, slots, send, recv, own):
+    scan, brick = lax.axis_index("scan"), lax.axis_index("ybrick")
+    mine_half, mine = brick // HALF, brick % HALF
+
+    def device(index):
+        return {"scan": scan, "ybrick": index}
+
+    barrier = pltpu.get_barrier_semaphore()
+    first = (BOTH_FIRST) * mine_half
+    last = BOTH_LAST + (BRICKS - 1 - BOTH_LAST) * mine_half
+
+    def greet(index, carry):
+        @pl.when(index != brick)
+        def _():
+            pl.semaphore_signal(barrier, inc=1, device_id=device(index), device_id_type=MESH)
+
+        return carry
+
+    lax.fori_loop(first, last + 1, greet, 0)
+    to_zero = (brick <= BOTH_LAST).astype(jnp.int32)
+    to_one = (brick >= BOTH_FIRST).astype(jnp.int32)
+    pl.semaphore_wait(barrier, HALF * (to_zero + to_one) - 1)
+
+    keep = pltpu.make_async_copy(raw.at[mine], slots.at[slot_of(brick, mine_half)], own)
+    keep.start()
+
+    def copy(step, half):
+        plane = lax.rem(mine + step, HALF)
+        slot = slot_of(brick, half)
+        return pltpu.make_async_remote_copy(
+            src_ref=raw.at[plane],
+            dst_ref=slots.at[slot],
+            send_sem=send.at[half, plane],
+            recv_sem=recv.at[slot],
+            device_id=device(half * HALF + plane),
+            device_id_type=MESH,
+        )
+
+    def each(act):
+        def body(step, carry):
+            for half, goes in ((0, to_zero), (1, to_one)):
+
+                @pl.when((goes == 1) & ((step > 0) | (mine_half != half)))
+                def _():
+                    act(copy(step, half))
+
+            return carry
+
+        lax.fori_loop(0, HALF, body, 0)
+
+    each(lambda one: one.start())
+
+    def arrive(index, carry):
+        @pl.when(index != brick)
+        def _():
+            slot = slot_of(index, mine_half)
+            pltpu.make_async_copy(slots.at[slot], slots.at[slot], recv.at[slot]).wait()
+
+        return carry
+
+    keep.wait()
+    lax.fori_loop(first, last + 1, arrive, 0)
+    each(lambda one: one.wait_send())
+
+
+def gather(raw):
+    return pl.pallas_call(
+        gather_kernel,
+        out_shape=jax.ShapeDtypeStruct((SLOTS, BRICK, COLS), jnp.bfloat16),
+        in_specs=[REFS],
+        out_specs=REFS,
+        scratch_shapes=[
+            pltpu.SemaphoreType.DMA((2, HALF)),
+            pltpu.SemaphoreType.DMA((SLOTS,)),
+            pltpu.SemaphoreType.DMA,
+        ],
+        compiler_params=pltpu.CompilerParams(collective_id=0, has_side_effects=True),
+    )(raw)
+
+
+def scatter_kernel(coded, whole, send, recv, own):
+    scan, spot = lax.axis_index("scan"), lax.axis_index("ybrick")
+    half, plane = spot // HALF, spot % HALF
+    group, place = plane // 4, lax.rem(plane, 4)
+    barrier = pltpu.get_barrier_semaphore()
+
+    def greet(index, carry):
+        source_scan, source_plane = index // 4, scan * 4 + lax.rem(index, 4)
+
+        @pl.when((source_scan != scan) | (source_plane != plane))
+        def _():
+            pl.semaphore_signal(
+                barrier,
+                inc=1,
+                device_id={"scan": source_scan, "ybrick": half * HALF + source_plane},
+                device_id_type=MESH,
+            )
+
+        return carry
+
+    lax.fori_loop(0, HALF, greet, 0)
+    stays = (group == scan).astype(jnp.int32)
+    pl.semaphore_wait(barrier, HALF - stays)
+
+    def target(place, scan):
+        return whole.at[place, :, pl.ds(pl.multiple_of(scan * COLS, COLS), COLS)]
+
+    def copy(step):
+        tile = lax.rem(plane + step, HALF)
+        return pltpu.make_async_remote_copy(
+            src_ref=coded.at[tile],
+            dst_ref=target(place, scan),
+            send_sem=send.at[tile],
+            recv_sem=recv.at[place, scan],
+            device_id={"scan": group, "ybrick": half * HALF + tile},
+            device_id_type=MESH,
+        )
+
+    keep = pltpu.make_async_copy(coded.at[plane], target(place, scan), own)
+
+    @pl.when(stays == 1)
+    def _():
+        keep.start()
+
+    def each(act):
+        def body(step, carry):
+            @pl.when((step > 0) | (stays == 0))
+            def _():
+                act(copy(step))
+
+            return carry
+
+        lax.fori_loop(0, HALF, body, 0)
+
+    each(lambda one: one.start())
+
+    @pl.when(stays == 1)
+    def _():
+        keep.wait()
+
+    def arrive(index, carry):
+        source_scan, slot = index // 4, lax.rem(index, 4)
+
+        @pl.when((source_scan != scan) | (scan * 4 + slot != plane))
+        def _():
+            pltpu.make_async_copy(target(slot, source_scan), target(slot, source_scan), recv.at[slot, source_scan]).wait()
+
+        return carry
+
+    lax.fori_loop(0, HALF, arrive, 0)
+    each(lambda one: one.wait_send())
+
+
+def scatter(coded):
+    return pl.pallas_call(
+        scatter_kernel,
+        out_shape=jax.ShapeDtypeStruct((4, BRICK, 4 * COLS), jnp.bfloat16),
+        in_specs=[REFS],
+        out_specs=REFS,
+        scratch_shapes=[
+            pltpu.SemaphoreType.DMA((HALF,)),
+            pltpu.SemaphoreType.DMA((4, 4)),
+            pltpu.SemaphoreType.DMA,
+        ],
+        compiler_params=pltpu.CompilerParams(collective_id=1, has_side_effects=True),
+    )(coded)
+
+
+def decode_kernel(coded, out):
+    out[...] = jnp.sqrt(coded[...].astype(jnp.float32))
+
+
+def decode(coded):
+    return pl.pallas_call(
+        decode_kernel,
+        grid=(8,),
+        out_shape=jax.ShapeDtypeStruct(coded.shape, jnp.float32),
+        in_specs=[pl.BlockSpec((4, 16, 4 * COLS), lambda i: (0, i, 0))],
+        out_specs=pl.BlockSpec((4, 16, 4 * COLS), lambda i: (0, i, 0)),
+    )(coded)
 
 
 SMEM = pl.BlockSpec(memory_space=pltpu.SMEM)
@@ -194,7 +384,7 @@
     scan = lax.axis_index("scan").astype(jnp.int32)
     spot = lax.axis_index("ybrick").astype(jnp.int32)
     half, plane = spot // HALF, spot % HALF
-    gathered = lax.all_to_all(jnp.concatenate([raw, raw], axis=0), "ybrick", split_axis=0, concat_axis=0, tiled=True)
+    gathered = gather(raw)
     shift = lax.dynamic_index_in_dim(row_shift, plane, keepdims=False)
     fraction = lax.dynamic_index_in_dim(frac_index, plane, keepdims=False)
     middle = deskew(half, shift, fraction, gathered)
@@ -203,10 +393,7 @@
     kernel_y = psf_y / jnp.sum(psf_y)
     kernel_x = psf_x / jnp.sum(psf_x)
     coded = deconvolve(half, scan, left, middle, right, kernel_y, kernel_x).reshape(HALF, BRICK, COLS)
-    groups = [list(range(HALF)), list(range(HALF, 2 * HALF))]
-    coded = lax.all_to_all(coded, "ybrick", split_axis=0, concat_axis=0, axis_index_groups=groups, tiled=True)
-    coded = lax.all_to_all(coded, "scan", split_axis=0, concat_axis=2, tiled=True)
-    return jnp.sqrt(coded.astype(jnp.float32))
+    return decode(scatter(coded))
 
 
 def solution(mesh):

time: 190 us -> 173 us (0.911)
  the two profiles are of different devices: /device:TPU:1 before, /device:TPU:120 now
where the time goes in v2:
time: 173 us; the launch traced here: 172 us
  Pallas kernels  149 us (86%)
  local copies, waits for them, and re-layouts  11.4 us (7%)
  starting transfers between devices  6.99 us (4%)
  other arithmetic  4.95 us (3%)
    pallas_call x1, Pallas kernels, gather(): pl.pallas_call(gather_kernel, out_shape=jax.ShapeDtypeStruct((SLOTS, BRIC...  68.4 us
    pallas_call x1, Pallas kernels, scatter(): pl.pallas_call(scatter_kernel, out_shape=jax.ShapeDtypeStruct((4, BRICK,...  44.4 us
    pallas_call x1, Pallas kernels, deconvolve(): pl.pallas_call(filter_kernel, out_shape=jax.ShapeDtypeStruct((HALF * BRIC...  22 us
    pallas_call x1, Pallas kernels, deskew(): pl.pallas_call(deskew_kernel, out_shape=jax.ShapeDtypeStruct((ROWS, COLS)...  7.57 us
    pallas_call x1, Pallas kernels, decode(): pl.pallas_call(decode_kernel, grid=(8,), out_shape=jax.ShapeDtypeStruct(c...  6.43 us
    ppermute x1, starting transfers between devices, local(): lax.ppermute(middle[:, :HALO], 'scan', [(i + 1, i) for i in range(3)])  5.07 us
  transfers between devices with their start and end apart: 2, of which 0 were waited for; matrix products, arithmetic and copies ran while one was open for 5% of the time, Pallas kernels for 0%

profile of v2, /device:TPU:120, one launch (start us, length us, event | category | flops | bytes accessed | tf_op | source)
XLA Modules:
  0.0 172.4 jit_solution(13242487028351454118)
XLA Ops:
  0.0 1.2 dynamic_slice.8
  1.2 1.3 dynamic_slice.7
  2.5 68.4 %shard_map.55.raw_ref = bf16[25,128,512]{2,1,0:T(8,128)(2,1)} custom-call(bf16[16,128,512]{2,1,0:T(8,128)(2,1)} %raw.1), custom_call_target="tpu_custom_call" | custom-call | tf_op jit(solution)/shard_map/pallas_call | solution.py:225
  71.0 1.9 %pad_add_fusion.1.scalars = s32[3]{0:T(128)} fusion(s32[1]{0:T(128)} %dynamic_slice.8, s32[1]{0:T(128)} %dynamic_slice.7, s32[1]{0:T(128)} %bitcast), kind=kLoop, calls=%fused_computation.7 | loop fusion | flops 6 | bytes 24 | tf_op jit(solution)/shard_map/stack | solution.py:353
  72.8 7.6 %shard_map.56.middle = bf16[2176,512]{1,0:T(8,128)(2,1)} custom-call(s32[3]{0:T(128)} %pad_add_fusion.1.scalars, bf16[25,128,512]{2,1,0:T(8,128)(2,1)} %shard_map.55.raw_ref), custom_call_target="tpu_custom_call" | custom-call | tf_op jit(solution)/shard_map/pallas_call | solution.py:346
  80.4 1.3 fusion
  81.8 5.1 %collective-permute-start.1 = (bf16[2176,128]{1,0:T(8,128)(2,1)S(1)}, bf16[2176,128]{1,0:T(8,128)(2,1)S(1)}, u32[]{:S(2)}, u32[]{:S(2)}) collective-permute-start(bf16[2176,128]{1,0:T(8,128)(2,1)S(1)} %get-tuple-element.5), channel_id=1, source_target_pairs={{32,0},{64,32},{96,64},{33,1},{65,33},{97,65},{34,2},{66,34},{98,6... | collective-permute-start | bytes 1671176 | tf_op jit(solution)/shard_map/ppermute | solution.py:392
  86.8 1.9 %collective-permute-start = (bf16[2176,128]{1,0:T(8,128)(2,1)S(1)}, bf16[2176,128]{1,0:T(8,128)(2,1)S(1)}, u32[]{:S(2)}, u32[]{:S(2)}) collective-permute-start(bf16[2176,128]{1,0:T(8,128)(2,1)S(1)} %get-tuple-element.6), channel_id=1, source_target_pairs={{0,32},{32,64},{64,96},{1,33},{33,65},{65,97},{2,34},{34,66},{66,9... | collective-permute-start | bytes 1671176 | tf_op jit(solution)/shard_map/ppermute | solution.py:391
  88.8 0.1 reverse.6
  88.9 0.6 reduce_sum.18
  89.5 0.6 reduce_sum.19
  90.1 0.1 reverse.7
  90.2 0.6 broadcast_divide_fusion.2
  90.9 0.4 tile.41
  91.3 0.7 convert_element_type.21.y_forward
  92.0 0.4 tile.43
  92.4 0.7 convert_element_type.22.y_back
  93.0 0.6 broadcast_divide_fusion
  93.7 0.6 tile.45
  94.3 0.3 reshape.19
  94.6 0.1 copy.6
  94.8 0.6 tile.47
  95.4 0.3 reshape.20
  95.8 0.1 copy.7
  95.9 0.6 pad_add_fusion.scalars
  96.5 0.7 pad_bitcast_fusion.1.x_forward
  97.2 0.7 pad_bitcast_fusion.x_back
  97.9 0.8 copy-done
  98.7 0.8 copy-done.1
  99.5 22.0 %shard_map.57 = bf16[2048,512]{1,0:T(8,128)(2,1)} custom-call(s32[2]{0:T(128)} %pad_add_fusion.scalars, bf16[2176,128]{1,0:T(8,128)(2,1)} %copy-done.1, bf16[2176,512]{1,0:T(8,128)(2,1)} %shard_map.56.middle, bf16[2176,128]{1,0:T(8,128)(2,1)} %copy-done, bf16[192,256]{1,0:T(8,128)(2,1)} %convert_element_type.21.y_forward, ...), custom_call_target="tpu_custom_call" | custom-call | tf_op jit(solution)/shard_map/pallas_call | solution.py:357
  121.5 44.4 %shard_map.58.coded = bf16[4,128,2048]{2,1,0:T(8,128)(2,1)} custom-call(bf16[16,128,512]{2,1,0:T(8,128)(2,1)} %bitcast.7), custom_call_target="tpu_custom_call" | custom-call | tf_op jit(solution)/shard_map/pallas_call | solution.py:313
  166.0 6.4 %shard_map.59 = f32[4,128,2048]{2,1,0:T(8,128)} custom-call(bf16[4,128,2048]{2,1,0:T(8,128)(2,1)} %shard_map.58.coded), custom_call_target="tpu_custom_call" | custom-call | tf_op jit(solution)/shard_map/pallas_call | solution.py:332
  (20 shorter events, 0.2 us)
Async XLA Ops:
  80.4 8.3 %copy-start.2 = (f32[65]{0:T(128)S(1)}, f32[65]{0:T(128)}, u32[]{:S(2)}) copy-start(f32[65]{0:T(128)} %param.8) | copy-start | bytes 784
  80.4 9.1 %copy-start.3 = (f32[65]{0:T(128)S(1)}, f32[65]{0:T(128)}, u32[]{:S(2)}) copy-start(f32[65]{0:T(128)} %param.9) | copy-start | bytes 784
  81.8 16.2 %collective-permute-start.1 = (bf16[2176,128]{1,0:T(8,128)(2,1)S(1)}, bf16[2176,128]{1,0:T(8,128)(2,1)S(1)}, u32[]{:S(2)}, u32[]{:S(2)}) collective-permute-start(bf16[2176,128]{1,0:T(8,128)(2,1)S(1)} %get-tuple-element.5), channel_id=1, source_target_pairs={{32,0},{64,32},{96,64},{33,1},{65,33},{97,65},{34,2},{66,34},{98,6... | collective-permute-start | bytes 1671176 | tf_op jit(solution)/shard_map/ppermute | solution.py:392
  86.8 11.1 %collective-permute-start = (bf16[2176,128]{1,0:T(8,128)(2,1)S(1)}, bf16[2176,128]{1,0:T(8,128)(2,1)S(1)}, u32[]{:S(2)}, u32[]{:S(2)}) collective-permute-start(bf16[2176,128]{1,0:T(8,128)(2,1)S(1)} %get-tuple-element.6), channel_id=1, source_target_pairs={{0,32},{32,64},{64,96},{1,33},{33,65},{65,97},{2,34},{34,66},{66,9... | collective-permute-start | bytes 1671176 | tf_op jit(solution)/shard_map/ppermute | solution.py:391
  97.9 0.8 copy-start
  98.7 0.8 copy-start.1

commit v3 on v1

v3 whole, which is shorter than its diff:
```python
import functools

import jax
import jax.numpy as jnp
from jax import lax
from jax.experimental import pallas as pl
from jax.experimental.pallas import tpu as pltpu
from jax.sharding import PartitionSpec as P

RADIUS = 32
TAPS = 2 * RADIUS + 1
NFRAC = 16
BRICK = 128
BRICKS = 32
ROWS = BRICK * BRICKS
REACH = 1024
PART = 256
HALO = 128
WIDE = PART + 2 * HALO
SPAN = BRICK + 2 * RADIUS
UNIT = 2
TALL = UNIT * BRICK
BLOCKS = BRICKS // UNIT
STRIDE = 7
TINY = 1e-30
MESH = pl.DeviceIdType.MESH
SMEM = pl.BlockSpec(memory_space=pltpu.SMEM)
VMEM = pl.BlockSpec(memory_space=pltpu.VMEM)
REFS = pl.BlockSpec(memory_space=pl.ANY)

background = 0.5


def spot_of(plane, side, scan):
    deep, down, high = plane // 8, (plane // 2) % 4, plane % 2
    return high * 16 + down * 4 + (2 * deep + scan + side) % 4


def work_of(scan, ybrick):
    turn = (ybrick % 4 - scan + 4) % 4
    return 8 * (turn // 2) + 2 * ((ybrick % 16) // 4) + ybrick // 16, turn % 2


def toeplitz(kernel, count_out, count_in):
    padded = jnp.pad(kernel, (0, count_in + 1 - TAPS))
    return jnp.tile(padded, count_out)[: count_out * count_in].reshape(count_out, count_in)


def rows_band(kernel):
    return toeplitz(kernel, BRICK, SPAN).astype(jnp.bfloat16)


def columns_band(kernel):
    band = toeplitz(kernel, PART, 416)
    return jnp.pad(band, ((0, 0), (96, 0))).T.astype(jnp.bfloat16)


def gather_kernel(raw, slots, send, recv, own):
    scan, brick = lax.axis_index("scan"), lax.axis_index("ybrick")
    barrier = pltpu.get_barrier_semaphore()

    def greet(step, carry):
        other = (brick + step) % BRICKS
        pl.semaphore_signal(barrier, inc=1, device_id={"ybrick": other}, device_id_type=MESH)
        return carry

    lax.fori_loop(1, BRICKS, greet, 0)
    pl.semaphore_wait(barrier, BRICKS - 1)

    def source(spot):
        plane, side = work_of(scan, spot)
        return raw.at[plane, :, pl.ds(pl.multiple_of(side * PART, PART), PART)]

    keep = pltpu.make_async_copy(source(brick), slots.at[brick], own)
    keep.start()

    def copy(step):
        spot = (brick + STRIDE * step) % BRICKS
        return pltpu.make_async_remote_copy(
            src_ref=source(spot),
            dst_ref=slots.at[brick],
            send_sem=send.at[spot],
            recv_sem=recv.at[brick],
            device_id={"ybrick": spot},
            device_id_type=MESH,
        )

    def start(step, carry):
        copy(step).start()
        return carry

    def arrive(step, carry):
        slot = (brick + step) % BRICKS
        pltpu.make_async_copy(slots.at[slot], slots.at[slot], recv.at[slot]).wait()
        return carry

    def sent(step, carry):
        copy(step).wait_send()
        return carry

    lax.fori_loop(1, BRICKS, start, 0)
    keep.wait()
    lax.fori_loop(1, BRICKS, arrive, 0)
    lax.fori_loop(1, BRICKS, sent, 0)


def gather(raw):
    return pl.pallas_call(
        gather_kernel,
        out_shape=jax.ShapeDtypeStruct((BRICKS, BRICK, PART), jnp.bfloat16),
        in_specs=[REFS],
        out_specs=REFS,
        scratch_shapes=[
            pltpu.SemaphoreType.DMA((BRICKS,)),
            pltpu.SemaphoreType.DMA((BRICKS,)),
            pltpu.SemaphoreType.DMA,
        ],
        compiler_params=pltpu.CompilerParams(collective_id=0, has_side_effects=True),
    )(raw)


def deskew_kernel(scalars, raw, out, buffer):
    shift = scalars[0]
    weight = scalars[1].astype(jnp.float32) / NFRAC

    def clear(k, carry):
        buffer[pl.ds(pl.multiple_of(k * BRICK, BRICK), BRICK), :] = jnp.zeros((BRICK, PART), jnp.float32)
        return carry

    def widen(k, carry):
        target = pl.ds(pl.multiple_of(REACH + k * BRICK, BRICK), BRICK)
        buffer[target, :] = raw[k].astype(jnp.float32)
        return carry

    def blend(k, carry):
        start = REACH + BRICK * k - shift - 1
        rest = lax.rem(start, 8)
        tall = BRICK + 16
        rows = buffer[pl.ds(pl.multiple_of(start - rest, 8), tall), :]
        lower = pltpu.roll(rows, lax.rem(tall - rest, tall), 0)[:BRICK]
        upper = pltpu.roll(rows, tall - 1 - rest, 0)[:BRICK]
        mixed = (1.0 - weight) * upper + weight * lower
        out[pl.ds(pl.multiple_of(k * BRICK, BRICK), BRICK), :] = mixed.astype(jnp.bfloat16)
        return carry

    lax.fori_loop(0, REACH // BRICK, clear, 0)
    lax.fori_loop(0, BRICKS, widen, 0)
    lax.fori_loop(0, BRICKS, blend, 0)


def deskew(shift, fraction, raw):
    return pl.pallas_call(
        deskew_kernel,
        out_shape=jax.ShapeDtypeStruct((ROWS, PART), jnp.bfloat16),
        in_specs=[SMEM, VMEM],
        out_specs=VMEM,
        scratch_shapes=[pltpu.VMEM((REACH + ROWS + 16, PART), jnp.float32)],
        compiler_params=pltpu.CompilerParams(vmem_limit_bytes=60 * 2**20),
    )(jnp.stack([shift, fraction]), raw)


def filter_kernel(
    middle, y_forward, y_back, x_forward, x_back, whole,
    observed, estimate, rounded, back, rows_done, ratio, coded, left, right,
    halo_send, halo_recv, send, recv, own,
):
    scan, spot = lax.axis_index("scan"), lax.axis_index("ybrick")
    plane, side = work_of(scan, spot)
    group, part = plane // 4, 2 * scan + side
    stays = (group == scan).astype(jnp.int32)
    first = ((plane % 4) * 8 + part) // UNIT
    has_left, has_right = part > 0, part < 7

    def owner(plane, part):
        return {"scan": part // 2, "ybrick": spot_of(plane, part % 2, part // 2)}

    barrier = pltpu.get_barrier_semaphore()

    def greet(index, carry):
        other, column = scan * 4 + index // 8, index % 8

        @pl.when((other != plane) | (column != part))
        def _():
            pl.semaphore_signal(barrier, inc=1, device_id=owner(other, column), device_id_type=MESH)

        return carry

    for there, step in ((has_left, -1), (has_right, 1)):

        @pl.when(there)
        def _():
            pl.semaphore_signal(barrier, inc=1, device_id=owner(plane, part + step), device_id_type=MESH)

    lax.fori_loop(0, BRICKS, greet, 0)
    pl.semaphore_wait(barrier, BRICKS - stays + has_left.astype(jnp.int32) + has_right.astype(jnp.int32))

    def block_at(turn):
        return (first + turn + BLOCKS) % BLOCKS

    def rows_of(block, offset=0):
        return pl.ds(pl.multiple_of(block * TALL + offset, RADIUS), TALL)

    def halo(block, to_right):
        edge = middle.at[rows_of(block), pl.ds(HALO if to_right else 0, HALO)]
        return pltpu.make_async_remote_copy(
            src_ref=edge,
            dst_ref=(left if to_right else right).at[rows_of(block), :],
            send_sem=halo_send.at[int(to_right), block],
            recv_sem=halo_recv.at[int(to_right), block],
            device_id=owner(plane, part + (1 if to_right else -1)),
            device_id_type=MESH,
        )

    def each_halo(act):
        def body(turn, carry):
            for there, to_right in ((has_left, False), (has_right, True)):

                @pl.when(there)
                def _():
                    act(halo(block_at(turn - 1), to_right))

            return carry

        lax.fori_loop(0, BLOCKS, body, 0)

    each_halo(lambda one: one.start())
    zeros = jnp.zeros((RADIUS, WIDE), jnp.bfloat16)
    for ref in (rounded, back):
        ref[pl.ds(0, RADIUS), :] = zeros
        ref[pl.ds(RADIUS + ROWS, RADIUS), :] = zeros

    def load(block):
        rows = rows_of(block)
        for ref, arrived, at, width, inside in (
            (middle, None, HALO, PART, None),
            (left, 1, 0, HALO, has_left),
            (right, 0, HALO + PART, HALO, has_right),
        ):
            if arrived is not None:

                @pl.when(inside)
                def _():
                    pltpu.make_async_copy(ref.at[rows, :], ref.at[rows, :], halo_recv.at[arrived, block]).wait()

            values = ref[rows, :].astype(jnp.float32) + background
            if inside is not None:
                values = jnp.where(inside, values, 0.0)
            observed[rows, pl.ds(at, width)] = values
            rounded[rows_of(block, RADIUS), pl.ds(at, width)] = values.astype(jnp.bfloat16)

    def dot(one, two):
        return jnp.dot(one, two, preferred_element_type=jnp.float32)

    def window(block, unit):
        return pl.ds(pl.multiple_of(block * TALL + unit * BRICK, BRICK), SPAN)

    blocks = ((0, 384, 128), (128, 512, 0))

    def ratios(block):
        for unit in range(UNIT):
            rows_done[pl.ds(unit * BRICK, BRICK), :] = dot(
                y_forward[...], rounded[window(block, unit), :]
            ).astype(jnp.bfloat16)
        for at, (low, high, offset) in enumerate(blocks):
            blurred = dot(rows_done[:, low:high], x_forward[offset : offset + high - low, :])
            cut = pl.ds(at * PART, PART)
            ratio[:, cut] = (observed[rows_of(block), cut] / jnp.maximum(blurred, TINY)).astype(jnp.bfloat16)

    def forward(block):
        ratios(block)
        for at, (low, high, offset) in enumerate(blocks):
            turned = dot(ratio[:, low:high], x_back[offset : offset + high - low, :])
            back[rows_of(block, RADIUS), pl.ds(at * PART, PART)] = turned.astype(jnp.bfloat16)

    def update(block):
        for unit in range(UNIT):
            rows = pl.ds(pl.multiple_of(block * TALL + unit * BRICK, BRICK), BRICK)
            fresh = observed[rows, :] * dot(y_back[...], back[window(block, unit), :])
            estimate[rows, :] = fresh[:, HALO : HALO + PART]
            target = pl.ds(pl.multiple_of(block * TALL + unit * BRICK + RADIUS, RADIUS), BRICK)
            rounded[target, :] = fresh.astype(jnp.bfloat16)

    def again(block):
        ratios(block)
        back[rows_of(block, RADIUS), pl.ds(HALO, PART)] = dot(ratio[...], x_back[...]).astype(jnp.bfloat16)

    def finish(block):
        for unit in range(UNIT):
            rows = pl.ds(pl.multiple_of(block * TALL + unit * BRICK, BRICK), BRICK)
            correction = dot(y_back[...], back[window(block, unit), pl.ds(HALO, PART)])
            final = estimate[rows, :] * correction
            coded[block * UNIT + unit] = (final * final).astype(jnp.bfloat16)

    def target(place, part):
        return whole.at[place, :, pl.ds(pl.multiple_of(part * PART, PART), PART)]

    keep = pltpu.make_async_copy(coded.at[spot], target(plane % 4, part), own)

    def leave(brick):
        return pltpu.make_async_remote_copy(
            src_ref=coded.at[brick],
            dst_ref=target(plane % 4, part),
            send_sem=send.at[brick],
            recv_sem=recv.at[plane % 4, part],
            device_id={"scan": group, "ybrick": brick},
            device_id_type=MESH,
        )

    def ship(block):
        for unit in range(UNIT):
            brick = block * UNIT + (unit + part) % UNIT
            away = (stays == 0) | (brick != spot)

            @pl.when(away)
            def _():
                leave(brick).start()

            @pl.when(jnp.logical_not(away))
            def _():
                keep.start()

    load(block_at(-1))
    load(block_at(0))

    def step(turn, carry):
        for stage, lag, begin, end in (
            (load, -1, 0, BLOCKS - 3),
            (forward, 0, 0, BLOCKS - 1),
            (update, 1, 2, BLOCKS + 1),
            (again, 2, 4, BLOCKS + 3),
            (ship, 4, 7, BLOCKS + 6),
            (finish, 3, 6, BLOCKS + 5),
        ):

            @pl.when((turn >= begin) & (turn <= end))
            def _():
                stage(block_at(turn - lag))

        return carry

    lax.fori_loop(0, BLOCKS + 7, step, 0)

    @pl.when(stays == 1)
    def _():
        keep.wait()

    def arrive(index, carry):
        other, column = scan * 4 + index // 8, index % 8

        @pl.when((other != plane) | (column != part))
        def _():
            ref = target(index // 8, column)
            pltpu.make_async_copy(ref, ref, recv.at[index // 8, column]).wait()

        return carry

    lax.fori_loop(0, BRICKS, arrive, 0)

    def sent(brick, carry):
        @pl.when((stays == 0) | (brick != spot))
        def _():
            leave(brick).wait_send()

        return carry

    lax.fori_loop(0, BRICKS, sent, 0)
    each_halo(lambda one: one.wait_send())


def deconvolve(middle, kernel_y, kernel_x):
    return pl.pallas_call(
        filter_kernel,
        out_shape=jax.ShapeDtypeStruct((4, BRICK, 8 * PART), jnp.bfloat16),
        in_specs=[VMEM] * 5,
        out_specs=REFS,
        scratch_shapes=[
            pltpu.VMEM((ROWS, WIDE), jnp.float32),
            pltpu.VMEM((ROWS, PART), jnp.float32),
            pltpu.VMEM((ROWS + 2 * RADIUS, WIDE), jnp.bfloat16),
            pltpu.VMEM((ROWS + 2 * RADIUS, WIDE), jnp.bfloat16),
            pltpu.VMEM((TALL, WIDE), jnp.bfloat16),
            pltpu.VMEM((TALL, WIDE), jnp.bfloat16),
            pltpu.VMEM((BRICKS, BRICK, PART), jnp.bfloat16),
            pltpu.VMEM((ROWS, HALO), jnp.bfloat16),
            pltpu.VMEM((ROWS, HALO), jnp.bfloat16),
            pltpu.SemaphoreType.DMA((2, BLOCKS)),
            pltpu.SemaphoreType.DMA((2, BLOCKS)),
            pltpu.SemaphoreType.DMA((BRICKS,)),
            pltpu.SemaphoreType.DMA((4, 8)),
            pltpu.SemaphoreType.DMA,
        ],
        compiler_params=pltpu.CompilerParams(
            collective_id=1, has_side_effects=True, vmem_limit_bytes=60 * 2**20
        ),
    )(
        middle,
        rows_band(kernel_y),
        rows_band(kernel_y[::-1]),
        columns_band(kernel_x),
        columns_band(kernel_x[::-1]),
    )


def decode_kernel(coded, out):
    values = coded[...].astype(jnp.float32)
    out[...] = values * lax.rsqrt(values)


def decode(coded):
    spec = pl.BlockSpec((4, 16, 8 * PART), lambda i: (0, i, 0))
    return pl.pallas_call(
        decode_kernel,
        grid=(BRICK // 16,),
        out_shape=jax.ShapeDtypeStruct(coded.shape, jnp.float32),
        in_specs=[spec],
        out_specs=spec,
    )(coded)


def local(raw, row_shift, frac_index, psf_y, psf_x):
    scan = lax.axis_index("scan").astype(jnp.int32)
    spot = lax.axis_index("ybrick").astype(jnp.int32)
    plane, _ = work_of(scan, spot)
    shift = lax.dynamic_index_in_dim(row_shift, plane, keepdims=False)
    fraction = lax.dynamic_index_in_dim(frac_index, plane, keepdims=False)
    middle = deskew(shift, fraction, gather(raw))
    kernel_y = psf_y / jnp.sum(psf_y)
    kernel_x = psf_x / jnp.sum(psf_x)
    return decode(deconvolve(middle, kernel_y, kernel_x))


def solution(mesh):
    return jax.shard_map(
        local,
        mesh=mesh,
        in_specs=(P(None, "ybrick", "scan"), P(), P(), P(), P()),
        out_specs=P("scan", "ybrick", None),
        check_vma=False,
    )
```

time: 190 us -> 128 us (0.67)
  the two profiles are of different devices: /device:TPU:1 before, /device:TPU:7 now
where the time goes in v3:
time: 128 us
  Pallas kernels  111 us (87%)
  local copies, waits for them, and re-layouts  9.72 us (8%)
  other arithmetic  7.09 us (6%)
    pallas_call x1, Pallas kernels, deconvolve(): pl.pallas_call(filter_kernel, out_shape=jax.ShapeDtypeStruct((4, BRICK, 8...  63.2 us
    pallas_call x1, Pallas kernels, gather(): pl.pallas_call(gather_kernel, out_shape=jax.ShapeDtypeStruct((BRICKS, BRI...  34.5 us
    pallas_call x1, Pallas kernels, deskew(): pl.pallas_call(deskew_kernel, out_shape=jax.ShapeDtypeStruct((ROWS, PART)...  6.9 us
    pallas_call x1, Pallas kernels, decode(): pl.pallas_call(decode_kernel, grid=(BRICK // 16,), out_shape=jax.ShapeDty...  6.18 us

profile of v3, /device:TPU:7, one launch (start us, length us, event | category | flops | bytes accessed | tf_op | source)
XLA Modules:
  0.0 127.7 jit_solution(17842154937387439095)
XLA Ops:
  0.0 1.3 %reduce_sum.19 = f32[]{:T(128)} reduce(f32[65]{0:T(128)} %param.9, f32[]{:T(128)} %constant.78.clone.1), dimensions={0}, to_apply=%region_1.2 | reduce | flops 64 | bytes 268 | tf_op jit(solution)/shard_map/reduce_sum | solution.py:428
  1.3 1.3 reduce_sum.18
  2.6 1.2 dynamic_slice.8
  3.8 1.3 dynamic_slice.7
  5.1 1.9 %pad_add_fusion.scalars = s32[2]{0:T(128)} fusion(s32[1]{0:T(128)} %dynamic_slice.8, s32[1]{0:T(128)} %dynamic_slice.7), kind=kLoop, calls=%fused_computation.6 | loop fusion | flops 2 | bytes 16 | tf_op jit(solution)/shard_map/stack | solution.py:159
  7.0 0.7 reverse.6
  7.8 1.2 broadcast_divide_fusion.2
  9.0 0.7 reverse.7
  9.8 1.4 %broadcast_divide_fusion = (bf16[65]{0:T(256)(128)(2,1)S(1)}, bf16[65]{0:T(256)(128)(2,1)S(1)}) fusion(f32[65]{0:T(128)S(1)} %reverse.7, f32[]{:T(128)} %reduce_sum.19, f32[65]{0:T(128)} %param.9), kind=kLoop, calls=%fused_computation.7 | loop fusion | flops 260 | bytes 784 | tf_op jit(solution)/shard_map/rev | solution.py:400
  11.1 0.3 tile.41
  11.5 0.7 convert_element_type.21.y_forward
  12.2 0.3 tile.43
  12.5 0.7 convert_element_type.22.y_back
  13.2 0.6 tile.45
  13.8 0.3 reshape.16
  14.2 0.1 copy.6
  14.3 0.7 pad_bitcast_fusion.1.x_forward
  15.1 0.6 tile.47
  15.7 0.3 reshape.17
  16.0 0.1 copy.7
  16.2 0.7 pad_bitcast_fusion.x_back
  16.9 34.5 %shard_map.55.raw = bf16[32,128,256]{2,1,0:T(8,128)(2,1)} custom-call(bf16[16,128,512]{2,1,0:T(8,128)(2,1)} %raw.1), custom_call_target="tpu_custom_call" | custom-call | tf_op jit(solution)/shard_map/pallas_call | solution.py:108
  51.4 6.9 %shard_map.56.middle = bf16[4096,256]{1,0:T(8,128)(2,1)} custom-call(s32[2]{0:T(128)} %pad_add_fusion.scalars, bf16[32,128,256]{2,1,0:T(8,128)(2,1)} %shard_map.55.raw), custom_call_target="tpu_custom_call" | custom-call | tf_op jit(solution)/shard_map/pallas_call | solution.py:152
  58.3 63.2 %shard_map.57.coded = bf16[4,128,2048]{2,1,0:T(8,128)(2,1)} custom-call(bf16[4096,256]{1,0:T(8,128)(2,1)} %shard_map.56.middle, bf16[128,192]{1,0:T(8,128)(2,1)} %convert_element_type.21.y_forward, bf16[128,192]{1,0:T(8,128)(2,1)} %convert_element_type.22.y_back, bf16[512,256]{1,0:T(8,128)(2,1)} %pad_bitcast_fusion.1.x_forward, ...), custom_call_target="tpu_custom_call" | custom-call | tf_op jit(solution)/shard_map/pallas_call | solution.py:371
  121.5 6.2 %shard_map.58 = f32[4,128,2048]{2,1,0:T(8,128)} custom-call(bf16[4,128,2048]{2,1,0:T(8,128)(2,1)} %shard_map.57.coded), custom_call_target="tpu_custom_call" | custom-call | tf_op jit(solution)/shard_map/pallas_call | solution.py:411
  (12 shorter events, 0.1 us)

commit v4 on v3

--- a/solution.py
+++ b/solution.py
@@ -41,21 +41,29 @@
     return 8 * (turn // 2) + 2 * ((ybrick % 16) // 4) + ybrick // 16, turn % 2
 
 
-def toeplitz(kernel, count_out, count_in):
-    padded = jnp.pad(kernel, (0, count_in + 1 - TAPS))
-    return jnp.tile(padded, count_out)[: count_out * count_in].reshape(count_out, count_in)
-
-
-def rows_band(kernel):
-    return toeplitz(kernel, BRICK, SPAN).astype(jnp.bfloat16)
-
-
-def columns_band(kernel):
-    band = toeplitz(kernel, PART, 416)
-    return jnp.pad(band, ((0, 0), (96, 0))).T.astype(jnp.bfloat16)
-
-
-def gather_kernel(raw, slots, send, recv, own):
+def start_of(scan, ybrick):
+    plane, side = work_of(scan, ybrick)
+    high, down = ybrick // 16, (ybrick // 4) % 2
+    return (5 * ((plane % 4) * 8 + 2 * scan + side)) % 32
+
+
+def spread(line, height, width, first):
+    rows = jnp.broadcast_to(line[:, :width], (height, width))
+    return pltpu.roll(rows, first % width, 1, stride=1, stride_axis=0)
+
+
+def bands(psf_y, psf_x, line, y_forward, y_back, x_forward, x_back):
+    line[...] = jnp.zeros_like(line)
+    line[:, :TAPS] = psf_y[...] / jnp.sum(psf_y[...], axis=1, keepdims=True)
+    y_forward[...] = spread(line, BRICK, 2 * BRICK, 0)[:, :SPAN].astype(jnp.bfloat16)
+    turned = spread(line, 2 * BRICK, 2 * BRICK, -2 * RADIUS)[:, :BRICK].T
+    y_back[...] = turned[:, :SPAN].astype(jnp.bfloat16)
+    line[:, :TAPS] = psf_x[...] / jnp.sum(psf_x[...], axis=1, keepdims=True)
+    x_forward[...] = spread(line, PART, WIDE, HALO - RADIUS).T.astype(jnp.bfloat16)
+    x_back[...] = spread(line, WIDE, WIDE, -(HALO + RADIUS))[:, :PART].astype(jnp.bfloat16)
+
+
+def gather_kernel(raw, psf_y, psf_x, slots, y_forward, y_back, x_forward, x_back, line, send, recv, own):
     scan, brick = lax.axis_index("scan"), lax.axis_index("ybrick")
     barrier = pltpu.get_barrier_semaphore()
 
@@ -99,29 +107,35 @@
         return carry
 
     lax.fori_loop(1, BRICKS, start, 0)
+    bands(psf_y, psf_x, line, y_forward, y_back, x_forward, x_back)
     keep.wait()
     lax.fori_loop(1, BRICKS, arrive, 0)
     lax.fori_loop(1, BRICKS, sent, 0)
 
 
-def gather(raw):
+def gather(raw, psf_y, psf_x):
     return pl.pallas_call(
         gather_kernel,
-        out_shape=jax.ShapeDtypeStruct((BRICKS, BRICK, PART), jnp.bfloat16),
-        in_specs=[REFS],
-        out_specs=REFS,
+        out_shape=[
+            jax.ShapeDtypeStruct(shape, jnp.bfloat16)
+            for shape in ((BRICKS, BRICK, PART), (BRICK, SPAN), (BRICK, SPAN), (WIDE, PART), (WIDE, PART))
+        ],
+        in_specs=[REFS, VMEM, VMEM],
+        out_specs=[REFS] + [VMEM] * 4,
         scratch_shapes=[
+            pltpu.VMEM((1, WIDE), jnp.float32),
             pltpu.SemaphoreType.DMA((BRICKS,)),
             pltpu.SemaphoreType.DMA((BRICKS,)),
             pltpu.SemaphoreType.DMA,
         ],
         compiler_params=pltpu.CompilerParams(collective_id=0, has_side_effects=True),
-    )(raw)
-
-
-def deskew_kernel(scalars, raw, out, buffer):
-    shift = scalars[0]
-    weight = scalars[1].astype(jnp.float32) / NFRAC
+    )(raw, psf_y.reshape(1, TAPS), psf_x.reshape(1, TAPS))
+
+
+def deskew_kernel(row_shift, frac_index, raw, out, buffer):
+    plane, _ = work_of(lax.axis_index("scan"), lax.axis_index("ybrick"))
+    shift = row_shift[plane]
+    weight = frac_index[plane].astype(jnp.float32) / NFRAC
 
     def clear(k, carry):
         buffer[pl.ds(pl.multiple_of(k * BRICK, BRICK), BRICK), :] = jnp.zeros((BRICK, PART), jnp.float32)
@@ -148,27 +162,28 @@
     lax.fori_loop(0, BRICKS, blend, 0)
 
 
-def deskew(shift, fraction, raw):
+def deskew(row_shift, frac_index, raw):
     return pl.pallas_call(
         deskew_kernel,
         out_shape=jax.ShapeDtypeStruct((ROWS, PART), jnp.bfloat16),
-        in_specs=[SMEM, VMEM],
+        in_specs=[SMEM, SMEM, VMEM],
         out_specs=VMEM,
         scratch_shapes=[pltpu.VMEM((REACH + ROWS + 16, PART), jnp.float32)],
         compiler_params=pltpu.CompilerParams(vmem_limit_bytes=60 * 2**20),
-    )(jnp.stack([shift, fraction]), raw)
+    )(row_shift, frac_index, raw)
 
 
 def filter_kernel(
     middle, y_forward, y_back, x_forward, x_back, whole,
-    observed, estimate, rounded, back, rows_done, ratio, coded, left, right,
+    observed, estimate, rounded, back, rounded_2, back_2, rows_done, ratio, rows_done_2, ratio_2,
+    coded, left, right,
     halo_send, halo_recv, send, recv, own,
 ):
     scan, spot = lax.axis_index("scan"), lax.axis_index("ybrick")
     plane, side = work_of(scan, spot)
     group, part = plane // 4, 2 * scan + side
     stays = (group == scan).astype(jnp.int32)
-    first = ((plane % 4) * 8 + part) // UNIT
+    first = start_of(scan, spot) // UNIT
     has_left, has_right = part > 0, part < 7
 
     def owner(plane, part):
@@ -200,14 +215,16 @@
     def rows_of(block, offset=0):
         return pl.ds(pl.multiple_of(block * TALL + offset, RADIUS), TALL)
 
-    def halo(block, to_right):
+    def halo(turn, to_right):
+        there = owner(plane, part + (1 if to_right else -1))
+        block = (start_of(there["scan"], there["ybrick"]) // UNIT + turn + BLOCKS) % BLOCKS
         edge = middle.at[rows_of(block), pl.ds(HALO if to_right else 0, HALO)]
         return pltpu.make_async_remote_copy(
             src_ref=edge,
             dst_ref=(left if to_right else right).at[rows_of(block), :],
             send_sem=halo_send.at[int(to_right), block],
             recv_sem=halo_recv.at[int(to_right), block],
-            device_id=owner(plane, part + (1 if to_right else -1)),
+            device_id=there,
             device_id_type=MESH,
         )
 
@@ -217,31 +234,32 @@
 
                 @pl.when(there)
                 def _():
-                    act(halo(block_at(turn - 1), to_right))
+                    act(halo(turn - 1, to_right))
 
             return carry
 
         lax.fori_loop(0, BLOCKS, body, 0)
 
     each_halo(lambda one: one.start())
-    zeros = jnp.zeros((RADIUS, WIDE), jnp.bfloat16)
-    for ref in (rounded, back):
-        ref[pl.ds(0, RADIUS), :] = zeros
-        ref[pl.ds(RADIUS + ROWS, RADIUS), :] = zeros
+    for ref in (rounded, back, rounded_2, back_2):
+        for edge in (pl.ds(0, RADIUS), pl.ds(RADIUS + ROWS, RADIUS)):
+            ref[edge, :] = jnp.zeros((RADIUS, ref.shape[1]), jnp.bfloat16)
+
+    def await_halo(block):
+        rows = rows_of(block)
+        for ref, arrived, inside in ((left, 1, has_left), (right, 0, has_right)):
+
+            @pl.when(inside)
+            def _():
+                pltpu.make_async_copy(ref.at[rows, :], ref.at[rows, :], halo_recv.at[arrived, block]).wait()
 
     def load(block):
         rows = rows_of(block)
-        for ref, arrived, at, width, inside in (
-            (middle, None, HALO, PART, None),
-            (left, 1, 0, HALO, has_left),
-            (right, 0, HALO + PART, HALO, has_right),
+        for ref, at, width, inside in (
+            (middle, HALO, PART, None),
+            (left, 0, HALO, has_left),
+            (right, HALO + PART, HALO, has_right),
         ):
-            if arrived is not None:
-
-                @pl.when(inside)
-                def _():
-                    pltpu.make_async_copy(ref.at[rows, :], ref.at[rows, :], halo_recv.at[arrived, block]).wait()
-
             values = ref[rows, :].astype(jnp.float32) + background
             if inside is not None:
                 values = jnp.where(inside, values, 0.0)
@@ -256,10 +274,10 @@
 
     blocks = ((0, 384, 128), (128, 512, 0))
 
-    def ratios(block):
+    def ratios(block, source, rows_done, ratio):
         for unit in range(UNIT):
             rows_done[pl.ds(unit * BRICK, BRICK), :] = dot(
-                y_forward[...], rounded[window(block, unit), :]
+                y_forward[...], source[window(block, unit), :]
             ).astype(jnp.bfloat16)
         for at, (low, high, offset) in enumerate(blocks):
             blurred = dot(rows_done[:, low:high], x_forward[offset : offset + high - low, :])
@@ -267,7 +285,7 @@
             ratio[:, cut] = (observed[rows_of(block), cut] / jnp.maximum(blurred, TINY)).astype(jnp.bfloat16)
 
     def forward(block):
-        ratios(block)
+        ratios(block, rounded, rows_done, ratio)
         for at, (low, high, offset) in enumerate(blocks):
             turned = dot(ratio[:, low:high], x_back[offset : offset + high - low, :])
             back[rows_of(block, RADIUS), pl.ds(at * PART, PART)] = turned.astype(jnp.bfloat16)
@@ -278,16 +296,16 @@
             fresh = observed[rows, :] * dot(y_back[...], back[window(block, unit), :])
             estimate[rows, :] = fresh[:, HALO : HALO + PART]
             target = pl.ds(pl.multiple_of(block * TALL + unit * BRICK + RADIUS, RADIUS), BRICK)
-            rounded[target, :] = fresh.astype(jnp.bfloat16)
+            rounded_2[target, :] = fresh.astype(jnp.bfloat16)
 
     def again(block):
-        ratios(block)
-        back[rows_of(block, RADIUS), pl.ds(HALO, PART)] = dot(ratio[...], x_back[...]).astype(jnp.bfloat16)
+        ratios(block, rounded_2, rows_done_2, ratio_2)
+        back_2[rows_of(block, RADIUS), :] = dot(ratio_2[...], x_back[...]).astype(jnp.bfloat16)
 
     def finish(block):
         for unit in range(UNIT):
             rows = pl.ds(pl.multiple_of(block * TALL + unit * BRICK, BRICK), BRICK)
-            correction = dot(y_back[...], back[window(block, unit), pl.ds(HALO, PART)])
+            correction = dot(y_back[...], back_2[window(block, unit), :])
             final = estimate[rows, :] * correction
             coded[block * UNIT + unit] = (final * final).astype(jnp.bfloat16)
 
@@ -308,7 +326,7 @@
 
     def ship(block):
         for unit in range(UNIT):
-            brick = block * UNIT + (unit + part) % UNIT
+            brick = block * UNIT + (unit + start_of(scan, spot)) % UNIT
             away = (stays == 0) | (brick != spot)
 
             @pl.when(away)
@@ -319,26 +337,29 @@
             def _():
                 keep.start()
 
-    load(block_at(-1))
-    load(block_at(0))
-
-    def step(turn, carry):
-        for stage, lag, begin, end in (
-            (load, -1, 0, BLOCKS - 3),
-            (forward, 0, 0, BLOCKS - 1),
-            (update, 1, 2, BLOCKS + 1),
-            (again, 2, 4, BLOCKS + 3),
-            (ship, 4, 7, BLOCKS + 6),
-            (finish, 3, 6, BLOCKS + 5),
-        ):
-
-            @pl.when((turn >= begin) & (turn <= end))
-            def _():
+    for turn in (-1, 0, 1):
+        await_halo(block_at(turn))
+        load(block_at(turn))
+
+    stages = (
+        (await_halo, -2, 0, BLOCKS - 4),
+        (ship, 7, 10, BLOCKS + 9),
+        (finish, 6, 9, BLOCKS + 8),
+        (again, 4, 6, BLOCKS + 5),
+        (update, 2, 3, BLOCKS + 2),
+        (forward, 0, 0, BLOCKS - 1),
+        (load, -2, 0, BLOCKS - 4),
+    )
+    cuts = sorted({begin for _, _, begin, _ in stages} | {end + 1 for _, _, _, end in stages})
+    for low, high in zip(cuts, cuts[1:]):
+        active = [(stage, lag) for stage, lag, begin, end in stages if begin <= low and low <= end]
+
+        def step(turn, carry):
+            for stage, lag in active:
                 stage(block_at(turn - lag))
-
-        return carry
-
-    lax.fori_loop(0, BLOCKS + 7, step, 0)
+            return carry
+
+        lax.fori_loop(low, high, step, 0)
 
     @pl.when(stays == 1)
     def _():
@@ -367,7 +388,7 @@
     each_halo(lambda one: one.wait_send())
 
 
-def deconvolve(middle, kernel_y, kernel_x):
+def deconvolve(middle, *matrices):
     return pl.pallas_call(
         filter_kernel,
         out_shape=jax.ShapeDtypeStruct((4, BRICK, 8 * PART), jnp.bfloat16),
@@ -378,6 +399,10 @@
             pltpu.VMEM((ROWS, PART), jnp.float32),
             pltpu.VMEM((ROWS + 2 * RADIUS, WIDE), jnp.bfloat16),
             pltpu.VMEM((ROWS + 2 * RADIUS, WIDE), jnp.bfloat16),
+            pltpu.VMEM((ROWS + 2 * RADIUS, WIDE), jnp.bfloat16),
+            pltpu.VMEM((ROWS + 2 * RADIUS, PART), jnp.bfloat16),
+            pltpu.VMEM((TALL, WIDE), jnp.bfloat16),
+            pltpu.VMEM((TALL, WIDE), jnp.bfloat16),
             pltpu.VMEM((TALL, WIDE), jnp.bfloat16),
             pltpu.VMEM((TALL, WIDE), jnp.bfloat16),
             pltpu.VMEM((BRICKS, BRICK, PART), jnp.bfloat16),
@@ -392,13 +417,7 @@
         compiler_params=pltpu.CompilerParams(
             collective_id=1, has_side_effects=True, vmem_limit_bytes=60 * 2**20
         ),
-    )(
-        middle,
-        rows_band(kernel_y),
-        rows_band(kernel_y[::-1]),
-        columns_band(kernel_x),
-        columns_band(kernel_x[::-1]),
-    )
+    )(middle, *matrices)
 
 
 def decode_kernel(coded, out):
@@ -418,15 +437,8 @@
 
 
 def local(raw, row_shift, frac_index, psf_y, psf_x):
-    scan = lax.axis_index("scan").astype(jnp.int32)
-    spot = lax.axis_index("ybrick").astype(jnp.int32)
-    plane, _ = work_of(scan, spot)
-    shift = lax.dynamic_index_in_dim(row_shift, plane, keepdims=False)
-    fraction = lax.dynamic_index_in_dim(frac_index, plane, keepdims=False)
-    middle = deskew(shift, fraction, gather(raw))
-    kernel_y = psf_y / jnp.sum(psf_y)
-    kernel_x = psf_x / jnp.sum(psf_x)
-    return decode(deconvolve(middle, kernel_y, kernel_x))
+    slots, *matrices = gather(raw, psf_y, psf_x)
+    return decode(deconvolve(deskew(row_shift, frac_index, slots), *matrices))
 
 
 def solution(mesh):

time: 128 us -> 109 us (0.85)
  the two profiles are of different devices: /device:TPU:7 before, /device:TPU:1 now
where the time goes in v4:
time: 109 us; the launch traced here: 108 us
  Pallas kernels  108 us (99%)
    pallas_call x1, Pallas kernels, deconvolve(): pl.pallas_call(filter_kernel, out_shape=jax.ShapeDtypeStruct((4, BRICK, 8...  58.2 us
    pallas_call x1, Pallas kernels, gather(): pl.pallas_call(gather_kernel, out_shape=[jax.ShapeDtypeStruct(shape, jnp....  36.9 us
    pallas_call x1, Pallas kernels, deskew(): pl.pallas_call(deskew_kernel, out_shape=jax.ShapeDtypeStruct((ROWS, PART)...  6.94 us
    pallas_call x1, Pallas kernels, decode(): pl.pallas_call(decode_kernel, grid=(BRICK // 16,), out_shape=jax.ShapeDty...  6.18 us

profile of v4, /device:TPU:1, one launch (start us, length us, event | category | flops | bytes accessed | tf_op | source)
XLA Modules:
  0.0 108.3 jit_solution(16299606230531947573)
XLA Ops:
  0.0 36.9 %shard_map.55 = (bf16[32,128,256]{2,1,0:T(8,128)(2,1)}, bf16[128,192]{1,0:T(8,128)(2,1)}, bf16[128,192]{1,0:T(8,128)(2,1)}, bf16[512,256]{1,0:T(8,128)(2,1)}, bf16[512,256]{1,0:T(8,128)(2,1)}) custom-call(bf16[16,128,512]{2,1,0:T(8,128)(2,1)} %raw.1, f32[1,65]{1,0:T(1,128)} %bitcast.2, f32[1,65]{1,0:T(1,128)} %bitcast.3), custom_call_target="tpu_custom_call" | custom-call | tf_op jit(solution)/shard_map/pallas_call | solution.py:117
  36.9 6.9 %shard_map.56.middle = bf16[4096,256]{1,0:T(8,128)(2,1)} custom-call(s32[16]{0:T(128)} %row_shift.1, s32[16]{0:T(128)} %frac_index.1, bf16[32,128,256]{2,1,0:T(8,128)(2,1)} %get-tuple-element.10.raw), custom_call_target="tpu_custom_call" | custom-call | tf_op jit(solution)/shard_map/pallas_call | solution.py:166
  43.9 58.2 %shard_map.57.coded = bf16[4,128,2048]{2,1,0:T(8,128)(2,1)} custom-call(bf16[4096,256]{1,0:T(8,128)(2,1)} %shard_map.56.middle, bf16[128,192]{1,0:T(8,128)(2,1)} %get-tuple-element.11.y_forward, bf16[128,192]{1,0:T(8,128)(2,1)} %get-tuple-element.12.y_back, bf16[512,256]{1,0:T(8,128)(2,1)} %get-tuple-element.13.x_forward, ...), custom_call_target="tpu_custom_call" | custom-call | tf_op jit(solution)/shard_map/pallas_call | solution.py:392
  102.1 6.2 %shard_map.58 = f32[4,128,2048]{2,1,0:T(8,128)} custom-call(bf16[4,128,2048]{2,1,0:T(8,128)(2,1)} %shard_map.57.coded), custom_call_target="tpu_custom_call" | custom-call | tf_op jit(solution)/shard_map/pallas_call | solution.py:430

commit v5 on v4

--- a/solution.py
+++ b/solution.py
@@ -44,7 +44,7 @@
 def start_of(scan, ybrick):
     plane, side = work_of(scan, ybrick)
     high, down = ybrick // 16, (ybrick // 4) % 2
-    return (5 * ((plane % 4) * 8 + 2 * scan + side)) % 32
+    return (plane % 4) * 8 + 2 * scan + side
 
 
 def spread(line, height, width, first):
@@ -63,121 +63,11 @@
     x_back[...] = spread(line, WIDE, WIDE, -(HALO + RADIUS))[:, :PART].astype(jnp.bfloat16)
 
 
-def gather_kernel(raw, psf_y, psf_x, slots, y_forward, y_back, x_forward, x_back, line, send, recv, own):
-    scan, brick = lax.axis_index("scan"), lax.axis_index("ybrick")
-    barrier = pltpu.get_barrier_semaphore()
-
-    def greet(step, carry):
-        other = (brick + step) % BRICKS
-        pl.semaphore_signal(barrier, inc=1, device_id={"ybrick": other}, device_id_type=MESH)
-        return carry
-
-    lax.fori_loop(1, BRICKS, greet, 0)
-    pl.semaphore_wait(barrier, BRICKS - 1)
-
-    def source(spot):
-        plane, side = work_of(scan, spot)
-        return raw.at[plane, :, pl.ds(pl.multiple_of(side * PART, PART), PART)]
-
-    keep = pltpu.make_async_copy(source(brick), slots.at[brick], own)
-    keep.start()
-
-    def copy(step):
-        spot = (brick + STRIDE * step) % BRICKS
-        return pltpu.make_async_remote_copy(
-            src_ref=source(spot),
-            dst_ref=slots.at[brick],
-            send_sem=send.at[spot],
-            recv_sem=recv.at[brick],
-            device_id={"ybrick": spot},
-            device_id_type=MESH,
-        )
-
-    def start(step, carry):
-        copy(step).start()
-        return carry
-
-    def arrive(step, carry):
-        slot = (brick + step) % BRICKS
-        pltpu.make_async_copy(slots.at[slot], slots.at[slot], recv.at[slot]).wait()
-        return carry
-
-    def sent(step, carry):
-        copy(step).wait_send()
-        return carry
-
-    lax.fori_loop(1, BRICKS, start, 0)
-    bands(psf_y, psf_x, line, y_forward, y_back, x_forward, x_back)
-    keep.wait()
-    lax.fori_loop(1, BRICKS, arrive, 0)
-    lax.fori_loop(1, BRICKS, sent, 0)
-
-
-def gather(raw, psf_y, psf_x):
-    return pl.pallas_call(
-        gather_kernel,
-        out_shape=[
-            jax.ShapeDtypeStruct(shape, jnp.bfloat16)
-            for shape in ((BRICKS, BRICK, PART), (BRICK, SPAN), (BRICK, SPAN), (WIDE, PART), (WIDE, PART))
-        ],
-        in_specs=[REFS, VMEM, VMEM],
-        out_specs=[REFS] + [VMEM] * 4,
-        scratch_shapes=[
-            pltpu.VMEM((1, WIDE), jnp.float32),
-            pltpu.SemaphoreType.DMA((BRICKS,)),
-            pltpu.SemaphoreType.DMA((BRICKS,)),
-            pltpu.SemaphoreType.DMA,
-        ],
-        compiler_params=pltpu.CompilerParams(collective_id=0, has_side_effects=True),
-    )(raw, psf_y.reshape(1, TAPS), psf_x.reshape(1, TAPS))
-
-
-def deskew_kernel(row_shift, frac_index, raw, out, buffer):
-    plane, _ = work_of(lax.axis_index("scan"), lax.axis_index("ybrick"))
-    shift = row_shift[plane]
-    weight = frac_index[plane].astype(jnp.float32) / NFRAC
-
-    def clear(k, carry):
-        buffer[pl.ds(pl.multiple_of(k * BRICK, BRICK), BRICK), :] = jnp.zeros((BRICK, PART), jnp.float32)
-        return carry
-
-    def widen(k, carry):
-        target = pl.ds(pl.multiple_of(REACH + k * BRICK, BRICK), BRICK)
-        buffer[target, :] = raw[k].astype(jnp.float32)
-        return carry
-
-    def blend(k, carry):
-        start = REACH + BRICK * k - shift - 1
-        rest = lax.rem(start, 8)
-        tall = BRICK + 16
-        rows = buffer[pl.ds(pl.multiple_of(start - rest, 8), tall), :]
-        lower = pltpu.roll(rows, lax.rem(tall - rest, tall), 0)[:BRICK]
-        upper = pltpu.roll(rows, tall - 1 - rest, 0)[:BRICK]
-        mixed = (1.0 - weight) * upper + weight * lower
-        out[pl.ds(pl.multiple_of(k * BRICK, BRICK), BRICK), :] = mixed.astype(jnp.bfloat16)
-        return carry
-
-    lax.fori_loop(0, REACH // BRICK, clear, 0)
-    lax.fori_loop(0, BRICKS, widen, 0)
-    lax.fori_loop(0, BRICKS, blend, 0)
-
-
-def deskew(row_shift, frac_index, raw):
-    return pl.pallas_call(
-        deskew_kernel,
-        out_shape=jax.ShapeDtypeStruct((ROWS, PART), jnp.bfloat16),
-        in_specs=[SMEM, SMEM, VMEM],
-        out_specs=VMEM,
-        scratch_shapes=[pltpu.VMEM((REACH + ROWS + 16, PART), jnp.float32)],
-        compiler_params=pltpu.CompilerParams(vmem_limit_bytes=60 * 2**20),
-    )(row_shift, frac_index, raw)
-
-
 def filter_kernel(
-    middle, y_forward, y_back, x_forward, x_back, whole,
+    raw, row_shift, frac_index, psf_y, psf_x, whole,
+    line, y_forward, y_back, x_forward, x_back, slots, moves, middle,
     observed, estimate, rounded, back, rounded_2, back_2, rows_done, ratio, rows_done_2, ratio_2,
-    coded, left, right,
-    halo_send, halo_recv, send, recv, own,
+    coded, left, right, raw_send, raw_recv, halo_send, halo_recv, send, recv, own,
 ):
     scan, spot = lax.axis_index("scan"), lax.axis_index("ybrick")
     plane, side = work_of(scan, spot)
@@ -206,8 +96,42 @@
         def _():
             pl.semaphore_signal(barrier, inc=1, device_id=owner(plane, part + step), device_id_type=MESH)
 
+    def greet_scan(step, carry):
+        other = (spot + step) % BRICKS
+        pl.semaphore_signal(barrier, inc=1, device_id={"ybrick": other}, device_id_type=MESH)
+        return carry
+
+    lax.fori_loop(1, BRICKS, greet_scan, 0)
     lax.fori_loop(0, BRICKS, greet, 0)
-    pl.semaphore_wait(barrier, BRICKS - stays + has_left.astype(jnp.int32) + has_right.astype(jnp.int32))
+    pl.semaphore_wait(barrier, 2 * BRICKS - 1 - stays + has_left.astype(jnp.int32) + has_right.astype(jnp.int32))
+
+    def source(there):
+        its_plane, its_side = work_of(scan, there)
+        return raw.at[its_plane, :, pl.ds(pl.multiple_of(its_side * PART, PART), PART)]
+
+    def tile_of(brick):
+        return slots.at[pl.ds(pl.multiple_of(REACH + brick * BRICK, BRICK), BRICK), :]
+
+    keep_raw = pltpu.make_async_copy(source(spot), tile_of(spot), own.at[0])
+    keep_raw.start()
+
+    def fetch(step):
+        there = (spot + STRIDE * step) % BRICKS
+        return pltpu.make_async_remote_copy(
+            src_ref=source(there),
+            dst_ref=tile_of(spot),
+            send_sem=raw_send.at[there],
+            recv_sem=raw_recv.at[spot],
+            device_id={"ybrick": there},
+            device_id_type=MESH,
+        )
+
+    def start_fetch(step, carry):
+        fetch(step).start()
+        return carry
+
+    lax.fori_loop(1, BRICKS, start_fetch, 0)
+    bands(psf_y, psf_x, line, y_forward, y_back, x_forward, x_back)
 
     def block_at(turn):
         return (first + turn + BLOCKS) % BLOCKS
@@ -215,35 +139,57 @@
     def rows_of(block, offset=0):
         return pl.ds(pl.multiple_of(block * TALL + offset, RADIUS), TALL)
 
-    def halo(turn, to_right):
-        there = owner(plane, part + (1 if to_right else -1))
-        block = (start_of(there["scan"], there["ybrick"]) // UNIT + turn + BLOCKS) % BLOCKS
+    def halo(block, to_right):
         edge = middle.at[rows_of(block), pl.ds(HALO if to_right else 0, HALO)]
         return pltpu.make_async_remote_copy(
             src_ref=edge,
             dst_ref=(left if to_right else right).at[rows_of(block), :],
             send_sem=halo_send.at[int(to_right), block],
             recv_sem=halo_recv.at[int(to_right), block],
-            device_id=there,
+            device_id=owner(plane, part + (1 if to_right else -1)),
             device_id_type=MESH,
         )
 
-    def each_halo(act):
-        def body(turn, carry):
-            for there, to_right in ((has_left, False), (has_right, True)):
-
-                @pl.when(there)
-                def _():
-                    act(halo(turn - 1, to_right))
-
-            return carry
-
-        lax.fori_loop(0, BLOCKS, body, 0)
-
-    each_halo(lambda one: one.start())
+    def both_halos(act, block):
+        for there, to_right in ((has_left, False), (has_right, True)):
+
+            @pl.when(there)
+            def _():
+                act(halo(block, to_right))
+
     for ref in (rounded, back, rounded_2, back_2):
         for edge in (pl.ds(0, RADIUS), pl.ds(RADIUS + ROWS, RADIUS)):
             ref[edge, :] = jnp.zeros((RADIUS, ref.shape[1]), jnp.bfloat16)
+
+    slots[pl.ds(0, REACH), :] = jnp.zeros((REACH, PART), jnp.bfloat16)
+    weight = frac_index[plane].astype(jnp.float32) / NFRAC
+    ahead = lax.broadcasted_iota(jnp.int32, moves.shape, 1) - lax.broadcasted_iota(jnp.int32, moves.shape, 0)
+    upper = jnp.where(ahead == REACH - row_shift[plane], 1.0 - weight, 0.0)
+    lower = jnp.where(ahead == REACH - 1 - row_shift[plane], weight, 0.0)
+    moves[...] = (upper + lower).astype(jnp.bfloat16)
+    keep_raw.wait()
+
+    def arrive_raw(step, carry):
+        brick = (spot - STRIDE * step + STRIDE * BRICKS) % BRICKS
+        pltpu.make_async_copy(tile_of(brick), tile_of(brick), raw_recv.at[brick]).wait()
+        return carry
+
+    lax.fori_loop(1, BRICKS, arrive_raw, 0)
+
+    def deskew(block):
+        for unit in range(UNIT):
+            begin = pl.multiple_of((block * UNIT + unit) * BRICK, BRICK)
+            mixed = jnp.dot(moves[...], slots[pl.ds(begin, REACH + BRICK), :], preferred_element_type=jnp.float32)
+            middle[pl.ds(begin, BRICK), :] = mixed.astype(jnp.bfloat16)
+
+    def deskew_turn(turn, carry):
+        both_halos(lambda one: one.start(), block_at(turn + BLOCKS - 3))
+        deskew(block_at(turn + BLOCKS - 2))
+        return carry
+
+    deskew(block_at(BLOCKS - 2))
+    lax.fori_loop(1, BLOCKS, deskew_turn, 0)
+    both_halos(lambda one: one.start(), block_at(BLOCKS - 3))
 
     def await_halo(block):
         rows = rows_of(block)
@@ -312,7 +258,7 @@
     def target(place, part):
         return whole.at[place, :, pl.ds(pl.multiple_of(part * PART, PART), PART)]
 
-    keep = pltpu.make_async_copy(coded.at[spot], target(plane % 4, part), own)
+    keep = pltpu.make_async_copy(coded.at[spot], target(plane % 4, part), own.at[1])
 
     def leave(brick):
         return pltpu.make_async_remote_copy(
@@ -385,39 +331,55 @@
         return carry
 
     lax.fori_loop(0, BRICKS, sent, 0)
-    each_halo(lambda one: one.wait_send())
-
-
-def deconvolve(middle, *matrices):
+
+    def sent_halo(block, carry):
+        both_halos(lambda one: one.wait_send(), block)
+        return carry
+
+    lax.fori_loop(0, BLOCKS, sent_halo, 0)
+
+    def sent_raw(step, carry):
+        fetch(step).wait_send()
+        return carry
+
+    lax.fori_loop(1, BRICKS, sent_raw, 0)
+
+
+def deconvolve(raw, row_shift, frac_index, psf_y, psf_x):
+    scratch = (
+        ((1, WIDE), jnp.float32),
+        ((BRICK, SPAN), jnp.bfloat16),
+        ((BRICK, SPAN), jnp.bfloat16),
+        ((WIDE, PART), jnp.bfloat16),
+        ((WIDE, PART), jnp.bfloat16),
+        ((REACH + ROWS, PART), jnp.bfloat16),
+        ((BRICK, REACH + BRICK), jnp.bfloat16),
+        ((ROWS, PART), jnp.bfloat16),
+        ((ROWS, WIDE), jnp.float32),
+        ((ROWS, PART), jnp.float32),
+        ((ROWS + 2 * RADIUS, WIDE), jnp.bfloat16),
+        ((ROWS + 2 * RADIUS, WIDE), jnp.bfloat16),
+        ((ROWS + 2 * RADIUS, WIDE), jnp.bfloat16),
+        ((ROWS + 2 * RADIUS, PART), jnp.bfloat16),
+        ((TALL, WIDE), jnp.bfloat16),
+        ((TALL, WIDE), jnp.bfloat16),
+        ((TALL, WIDE), jnp.bfloat16),
+        ((TALL, WIDE), jnp.bfloat16),
+        ((BRICKS, BRICK, PART), jnp.bfloat16),
+        ((ROWS, HALO), jnp.bfloat16),
+        ((ROWS, HALO), jnp.bfloat16),
+    )
+    semaphores = ((BRICKS,), (BRICKS,), (2, BLOCKS), (2, BLOCKS), (BRICKS,), (4, 8), (2,))
     return pl.pallas_call(
         filter_kernel,
         out_shape=jax.ShapeDtypeStruct((4, BRICK, 8 * PART), jnp.bfloat16),
-        in_specs=[VMEM] * 5,
+        in_specs=[REFS, SMEM, SMEM, VMEM, VMEM],
         out_specs=REFS,
-        scratch_shapes=[
-            pltpu.VMEM((ROWS, WIDE), jnp.float32),
-            pltpu.VMEM((ROWS, PART), jnp.float32),
-            pltpu.VMEM((ROWS + 2 * RADIUS, WIDE), jnp.bfloat16),
-            pltpu.VMEM((ROWS + 2 * RADIUS, WIDE), jnp.bfloat16),
-            pltpu.VMEM((ROWS + 2 * RADIUS, WIDE), jnp.bfloat16),
-            pltpu.VMEM((ROWS + 2 * RADIUS, PART), jnp.bfloat16),
-            pltpu.VMEM((TALL, WIDE), jnp.bfloat16),
-            pltpu.VMEM((TALL, WIDE), jnp.bfloat16),
-            pltpu.VMEM((TALL, WIDE), jnp.bfloat16),
-            pltpu.VMEM((TALL, WIDE), jnp.bfloat16),
-            pltpu.VMEM((BRICKS, BRICK, PART), jnp.bfloat16),
-            pltpu.VMEM((ROWS, HALO), jnp.bfloat16),
-            pltpu.VMEM((ROWS, HALO), jnp.bfloat16),
-            pltpu.SemaphoreType.DMA((2, BLOCKS)),
-            pltpu.SemaphoreType.DMA((2, BLOCKS)),
-            pltpu.SemaphoreType.DMA((BRICKS,)),
-            pltpu.SemaphoreType.DMA((4, 8)),
-            pltpu.SemaphoreType.DMA,
-        ],
+        scratch_shapes=[pltpu.VMEM(*one) for one in scratch] + [pltpu.SemaphoreType.DMA(one) for one in semaphores],
         compiler_params=pltpu.CompilerParams(
-            collective_id=1, has_side_effects=True, vmem_limit_bytes=60 * 2**20
+            collective_id=0, has_side_effects=True, vmem_limit_bytes=60 * 2**20
         ),
-    )(middle, *matrices)
+    )(raw, row_shift, frac_index, psf_y.reshape(1, TAPS), psf_x.reshape(1, TAPS))
 
 
 def decode_kernel(coded, out):
@@ -437,8 +399,7 @@
 
 
 def local(raw, row_shift, frac_index, psf_y, psf_x):
-    slots, *matrices = gather(raw, psf_y, psf_x)
-    return decode(deconvolve(deskew(row_shift, frac_index, slots), *matrices))
+    return decode(deconvolve(raw, row_shift, frac_index, psf_y, psf_x))
 
 
 def solution(mesh):

time: 109 us -> 97.2 us (0.89)
  Pallas kernels: 108 us -> 96.2 us
    pallas_call x2 -> x0, Pallas kernels: 43.9 us -> none  [the longest x1 36.9 us: gather(): pl.pallas_call(gather_kernel, out_shape=[jax.ShapeDtypeStruct(shape, jnp....]
    pallas_call x1, Pallas kernels: 58.2 us -> 90.1 us  [deconvolve(): pl.pallas_call(filter_kernel, out_shape=jax.ShapeDtypeStruct((4, BRICK, 8...]
where the time goes in v5:
time: 97.2 us; the launch traced here: 96.3 us
  Pallas kernels  96.2 us (99%)
    pallas_call x1, Pallas kernels, deconvolve(): pl.pallas_call(filter_kernel, out_shape=jax.ShapeDtypeStruct((4, BRICK, 8...  90.1 us
    pallas_call x1, Pallas kernels, decode(): pl.pallas_call(decode_kernel, grid=(BRICK // 16,), out_shape=jax.ShapeDty...  6.18 us

profile of v5, /device:TPU:1, one launch (start us, length us, event | category | flops | bytes accessed | tf_op | source)
XLA Modules:
  0.0 96.3 jit_solution(9906594603789075247)
XLA Ops:
  0.0 90.1 %shard_map.55.coded = bf16[4,128,2048]{2,1,0:T(8,128)(2,1)} custom-call(bf16[16,128,512]{2,1,0:T(8,128)(2,1)} %raw.1, s32[16]{0:T(128)} %row_shift.1, s32[16]{0:T(128)} %frac_index.1, f32[1,65]{1,0:T(1,128)} %bitcast.2, f32[1,65]{1,0:T(1,128)} %bitcast.3), custom_call_target="tpu_custom_call" | custom-call | tf_op jit(solution)/shard_map/pallas_call | solution.py:373
  90.1 6.2 %shard_map.56 = f32[4,128,2048]{2,1,0:T(8,128)} custom-call(bf16[4,128,2048]{2,1,0:T(8,128)(2,1)} %shard_map.55.coded), custom_call_target="tpu_custom_call" | custom-call | tf_op jit(solution)/shard_map/pallas_call | solution.py:392

commit v6 on v5

--- a/solution.py
+++ b/solution.py
@@ -189,7 +189,7 @@
 
     deskew(block_at(BLOCKS - 2))
     lax.fori_loop(1, BLOCKS, deskew_turn, 0)
-    both_halos(lambda one: one.start(), block_at(BLOCKS - 3))
+    both_halos(lambda one: one.start(), block_at(2 * BLOCKS - 3))
 
     def await_halo(block):
         rows = rows_of(block)
@@ -382,19 +382,42 @@
     )(raw, row_shift, frac_index, psf_y.reshape(1, TAPS), psf_x.reshape(1, TAPS))
 
 
-def decode_kernel(coded, out):
-    values = coded[...].astype(jnp.float32)
-    out[...] = values * lax.rsqrt(values)
+PIECES = 8
+
+
+def decode_kernel(coded, out, before, after, arrive, leave):
+    tall = 4 * BRICK // PIECES
+
+    def piece(ref, k):
+        return ref.at[k * tall // BRICK, pl.ds(k * tall % BRICK, tall), :]
+
+    reads = [pltpu.make_async_copy(piece(coded, k), before.at[k], arrive.at[k]) for k in range(PIECES)]
+    writes = [pltpu.make_async_copy(after.at[k], piece(out, k), leave.at[k]) for k in range(PIECES)]
+    for read in reads:
+        read.start()
+    for k in range(PIECES):
+        reads[k].wait()
+        values = before[k].astype(jnp.float32)
+        after[k] = values * lax.rsqrt(values)
+        writes[k].start()
+    for write in writes:
+        write.wait()
 
 
 def decode(coded):
-    spec = pl.BlockSpec((4, 16, 8 * PART), lambda i: (0, i, 0))
+    shape = (PIECES, 4 * BRICK // PIECES, 8 * PART)
     return pl.pallas_call(
         decode_kernel,
-        grid=(BRICK // 16,),
         out_shape=jax.ShapeDtypeStruct(coded.shape, jnp.float32),
-        in_specs=[spec],
-        out_specs=spec,
+        in_specs=[REFS],
+        out_specs=REFS,
+        scratch_shapes=[
+            pltpu.VMEM(shape, jnp.bfloat16),
+            pltpu.VMEM(shape, jnp.float32),
+            pltpu.SemaphoreType.DMA((PIECES,)),
+            pltpu.SemaphoreType.DMA((PIECES,)),
+        ],
+        compiler_params=pltpu.CompilerParams(vmem_limit_bytes=60 * 2**20),
     )(coded)
 
 

time: 97.2 us -> 94.1 us (0.968)
  Pallas kernels: 96.2 us -> 93.2 us
    pallas_call x1, Pallas kernels: 6.18 us -> 3.17 us  [decode(): pl.pallas_call(decode_kernel, out_shape=jax.ShapeDtypeStruct(coded.shape,...]
where the time goes in v6:
time: 94.1 us; the launch traced here: 93.2 us
  Pallas kernels  93.2 us (99%)
    pallas_call x1, Pallas kernels, deconvolve(): pl.pallas_call(filter_kernel, out_shape=jax.ShapeDtypeStruct((4, BRICK, 8...  90.1 us
    pallas_call x1, Pallas kernels, decode(): pl.pallas_call(decode_kernel, out_shape=jax.ShapeDtypeStruct(coded.shape,...  3.17 us

profile of v6, /device:TPU:1, one launch (start us, length us, event | category | flops | bytes accessed | tf_op | source)
XLA Modules:
  0.0 93.2 jit_solution(4892849737184341853)
XLA Ops:
  0.0 90.1 %shard_map.55.coded = bf16[4,128,2048]{2,1,0:T(8,128)(2,1)} custom-call(bf16[16,128,512]{2,1,0:T(8,128)(2,1)} %raw.1, s32[16]{0:T(128)} %row_shift.1, s32[16]{0:T(128)} %frac_index.1, f32[1,65]{1,0:T(1,128)} %bitcast.2, f32[1,65]{1,0:T(1,128)} %bitcast.3), custom_call_target="tpu_custom_call" | custom-call | tf_op jit(solution)/shard_map/pallas_call | solution.py:373
  90.1 3.2 %shard_map.56 = f32[4,128,2048]{2,1,0:T(8,128)} custom-call(bf16[4,128,2048]{2,1,0:T(8,128)(2,1)} %shard_map.55.coded), custom_call_target="tpu_custom_call" | custom-call | tf_op jit(solution)/shard_map/pallas_call | solution.py:409

commit v7 on v6

--- a/solution.py
+++ b/solution.py
@@ -81,15 +81,6 @@
 
     barrier = pltpu.get_barrier_semaphore()
 
-    def greet(index, carry):
-        other, column = scan * 4 + index // 8, index % 8
-
-        @pl.when((other != plane) | (column != part))
-        def _():
-            pl.semaphore_signal(barrier, inc=1, device_id=owner(other, column), device_id_type=MESH)
-
-        return carry
-
     for there, step in ((has_left, -1), (has_right, 1)):
 
         @pl.when(there)
@@ -102,7 +93,18 @@
         return carry
 
     lax.fori_loop(1, BRICKS, greet_scan, 0)
-    lax.fori_loop(0, BRICKS, greet, 0)
+    for from_scan in range(4):
+        for turned in range(2):
+            column = 2 * from_scan + turned
+            deep = (2 * (scan // 2) + from_scan + turned) % 4
+            for place in range(4):
+                there = (place % 2) * 16 + (2 * (scan % 2) + place // 2) * 4 + deep
+
+                @pl.when((from_scan != scan) | (there != spot))
+                def _():
+                    device = {"scan": from_scan, "ybrick": there}
+                    pl.semaphore_signal(barrier, inc=1, device_id=device, device_id_type=MESH)
+
     pl.semaphore_wait(barrier, 2 * BRICKS - 1 - stays + has_left.astype(jnp.int32) + has_right.astype(jnp.int32))
 
     def source(there):
@@ -307,21 +309,13 @@
 
         lax.fori_loop(low, high, step, 0)
 
-    @pl.when(stays == 1)
-    def _():
-        keep.wait()
-
-    def arrive(index, carry):
-        other, column = scan * 4 + index // 8, index % 8
-
-        @pl.when((other != plane) | (column != part))
-        def _():
-            ref = target(index // 8, column)
-            pltpu.make_async_copy(ref, ref, recv.at[index // 8, column]).wait()
-
-        return carry
-
-    lax.fori_loop(0, BRICKS, arrive, 0)
+    def sent_raw(step, carry):
+        fetch(step).wait_send()
+        return carry
+
+    def sent_halo(block, carry):
+        both_halos(lambda one: one.wait_send(), block)
+        return carry
 
     def sent(brick, carry):
         @pl.when((stays == 0) | (brick != spot))
@@ -330,19 +324,21 @@
 
         return carry
 
+    lax.fori_loop(1, BRICKS, sent_raw, 0)
+    lax.fori_loop(0, BLOCKS, sent_halo, 0)
+
+    @pl.when(stays == 1)
+    def _():
+        keep.wait()
+
     lax.fori_loop(0, BRICKS, sent, 0)
-
-    def sent_halo(block, carry):
-        both_halos(lambda one: one.wait_send(), block)
-        return carry
-
-    lax.fori_loop(0, BLOCKS, sent_halo, 0)
-
-    def sent_raw(step, carry):
-        fetch(step).wait_send()
-        return carry
-
-    lax.fori_loop(1, BRICKS, sent_raw, 0)
+    for place in range(4):
+        for column in range(8):
+
+            @pl.when((stays == 0) | (place != plane % 4) | (column != part))
+            def _():
+                ref = target(place, column)
+                pltpu.make_async_copy(ref, ref, recv.at[place, column]).wait()
 
 
 def deconvolve(raw, row_shift, frac_index, psf_y, psf_x):

time: 94.1 us -> 92.6 us (0.984)
  Pallas kernels: 93.2 us -> 90.8 us
    pallas_call x1, Pallas kernels: 90.1 us -> 87.6 us  [deconvolve(): pl.pallas_call(filter_kernel, out_shape=jax.ShapeDtypeStruct((4, BRICK, 8...]
where the time goes in v7:
time: 92.6 us; the launch traced here: 90.8 us
  Pallas kernels  90.8 us (98%)
    pallas_call x1, Pallas kernels, deconvolve(): pl.pallas_call(filter_kernel, out_shape=jax.ShapeDtypeStruct((4, BRICK, 8...  87.6 us
    pallas_call x1, Pallas kernels, decode(): pl.pallas_call(decode_kernel, out_shape=jax.ShapeDtypeStruct(coded.shape,...  3.17 us

profile of v7, /device:TPU:1, one launch (start us, length us, event | category | flops | bytes accessed | tf_op | source)
XLA Modules:
  0.0 90.8 jit_solution(2737176930851366622)
XLA Ops:
  0.0 87.6 %shard_map.55.coded = bf16[4,128,2048]{2,1,0:T(8,128)(2,1)} custom-call(bf16[16,128,512]{2,1,0:T(8,128)(2,1)} %raw.1, s32[16]{0:T(128)} %row_shift.1, s32[16]{0:T(128)} %frac_index.1, f32[1,65]{1,0:T(1,128)} %bitcast.2, f32[1,65]{1,0:T(1,128)} %bitcast.3), custom_call_target="tpu_custom_call" | custom-call | tf_op jit(solution)/shard_map/pallas_call | solution.py:369
  87.6 3.2 %shard_map.56 = f32[4,128,2048]{2,1,0:T(8,128)} custom-call(bf16[4,128,2048]{2,1,0:T(8,128)(2,1)} %shard_map.55.coded), custom_call_target="tpu_custom_call" | custom-call | tf_op jit(solution)/shard_map/pallas_call | solution.py:405

commit v8 on v7

--- a/solution.py
+++ b/solution.py
@@ -184,14 +184,18 @@
             mixed = jnp.dot(moves[...], slots[pl.ds(begin, REACH + BRICK), :], preferred_element_type=jnp.float32)
             middle[pl.ds(begin, BRICK), :] = mixed.astype(jnp.bfloat16)
 
-    def deskew_turn(turn, carry):
-        both_halos(lambda one: one.start(), block_at(turn + BLOCKS - 3))
-        deskew(block_at(turn + BLOCKS - 2))
-        return carry
-
-    deskew(block_at(BLOCKS - 2))
-    lax.fori_loop(1, BLOCKS, deskew_turn, 0)
-    both_halos(lambda one: one.start(), block_at(2 * BLOCKS - 3))
+    def deskew_four(turn, carry):
+        for at in range(4):
+            both_halos(lambda one: one.start(), block_at(4 * turn + at + BLOCKS - 6))
+        for at in range(4):
+            deskew(block_at(4 * turn + at + BLOCKS - 2))
+        return carry
+
+    for at in range(4):
+        deskew(block_at(at + BLOCKS - 2))
+    lax.fori_loop(1, BLOCKS // 4, deskew_four, 0)
+    for at in range(4):
+        both_halos(lambda one: one.start(), block_at(at + 2 * BLOCKS - 6))
 
     def await_halo(block):
         rows = rows_of(block)

time: 92.6 us -> 93.4 us (level)
  Pallas kernels: 90.8 us -> 92 us
    pallas_call x1, Pallas kernels: 87.6 us -> 88.9 us  [deconvolve(): pl.pallas_call(filter_kernel, out_shape=jax.ShapeDtypeStruct((4, BRICK, 8...]
where the time goes in v8:
time: 93.4 us; the launch traced here: 92 us
  Pallas kernels  92 us (99%)
    pallas_call x1, Pallas kernels, deconvolve(): pl.pallas_call(filter_kernel, out_shape=jax.ShapeDtypeStruct((4, BRICK, 8...  88.9 us
    pallas_call x1, Pallas kernels, decode(): pl.pallas_call(decode_kernel, out_shape=jax.ShapeDtypeStruct(coded.shape,...  3.17 us

profile of v8, /device:TPU:1, one launch (start us, length us, event | category | flops | bytes accessed | tf_op | source)
XLA Modules:
  0.0 92.0 jit_solution(394931332773634680)
XLA Ops:
  0.0 88.9 %shard_map.55.coded = bf16[4,128,2048]{2,1,0:T(8,128)(2,1)} custom-call(bf16[16,128,512]{2,1,0:T(8,128)(2,1)} %raw.1, s32[16]{0:T(128)} %row_shift.1, s32[16]{0:T(128)} %frac_index.1, f32[1,65]{1,0:T(1,128)} %bitcast.2, f32[1,65]{1,0:T(1,128)} %bitcast.3), custom_call_target="tpu_custom_call" | custom-call | tf_op jit(solution)/shard_map/pallas_call | solution.py:373
  88.9 3.2 %shard_map.56 = f32[4,128,2048]{2,1,0:T(8,128)} custom-call(bf16[4,128,2048]{2,1,0:T(8,128)(2,1)} %shard_map.55.coded), custom_call_target="tpu_custom_call" | custom-call | tf_op jit(solution)/shard_map/pallas_call | solution.py:409
